TPU v7x, 128 devices: a whole 4x4x4 slice. The times are simulated.
128 devices in a mesh: fsdp: 16 (over z, x_lo, core), tp: 8 (over x_hi, y).
Axes of the slice: x: 4 (x_hi: 2, x_lo: 2; x = x_hi * 2 + x_lo), y: 4, z: 4, core: 2. Of those that a mesh axis runs over, the one named last changes fastest.
Arguments:
- states: bfloat16 [512, 4, 8192], P('fsdp'), may hold values from -6 to 6
- norm_gain: float32 [8192], replicated, may hold values from 0.5 to 1.5
- query_base: bfloat16 [8192, 8192], P(('fsdp', 'tp')), may hold values from -0.0625 to 0.0625
- key_base: bfloat16 [8192, 1024], P(('fsdp', 'tp')), may hold values from -0.0625 to 0.0625
- value_base: bfloat16 [8192, 1024], P(('fsdp', 'tp')), may hold values from -0.0625 to 0.0625
- output_base: bfloat16 [8192, 8192], P(('fsdp', 'tp')), may hold values from -0.5 to 0.5
- query_down: bfloat16 [4, 8192, 64], P(None, ('fsdp', 'tp')), may hold values from -0.0625 to 0.0625
- query_up: bfloat16 [4, 64, 8192], replicated, may hold values from -0.75 to 0.75
- key_down: bfloat16 [4, 8192, 64], P(None, ('fsdp', 'tp')), may hold values from -0.0625 to 0.0625
- key_up: bfloat16 [4, 64, 1024], replicated, may hold values from -0.75 to 0.75
- value_down: bfloat16 [4, 8192, 64], P(None, ('fsdp', 'tp')), may hold values from -0.0625 to 0.0625
- value_up: bfloat16 [4, 64, 1024], replicated, may hold values from -0.75 to 0.75
- output_down: bfloat16 [4, 8192, 64], P(None, ('fsdp', 'tp')), may hold values from -0.5 to 0.5
- output_up: bfloat16 [4, 64, 8192], replicated, may hold values from -0.75 to 0.75
- adapter_layer: int32 [1], replicated, may hold values from 0 to 3
- kv_lengths: int32 [512], P('fsdp'), may hold values from 8 to 512
- cache_keys: bfloat16 [512, 512, 8, 128], P('fsdp', None, 'tp'), may hold values from -320 to 320
- cache_values: bfloat16 [512, 512, 8, 128], P('fsdp', None, 'tp'), may hold values from -6 to 6
Outputs:
- layer_update: bfloat16 [512, 4, 8192], P('fsdp', None, 'tp')
Inputs may be any that keep to these rules, and one draw needn't show every extreme that they name: `kv_lengths`: slots at and beyond a sequence's length hold no cached position.
All inputs are finite; a program needn't handle non-finite values.
Results may differ from a plain program's by a relative error of at most 0.012.
The roundings to bfloat16 on the way count: a program that leaves them out, or rounds other values in their place, can miss the bound.
Values may be sent and summed in bfloat16 or wider, within the bound.
A program may use at most 128 MiB of HBM per device.

v0:
```python
import jax
import jax.numpy as jnp
from jax import lax
from jax.sharding import PartitionSpec as P

HQ = 64
KVH = 8
DH = 128


rope_theta = 1000000.0
low_rank_scale = 0.5
epsilon = 1e-06


def sent_to_all(array, axis):
    copies = jnp.broadcast_to(array, (lax.axis_size(axis), *array.shape))
    return lax.all_to_all(copies, axis, split_axis=0, concat_axis=0, tiled=True)


def joined_along(tiles, dim):
    tiles = jnp.moveaxis(tiles, 0, dim)
    shape = tiles.shape
    return tiles.reshape(*shape[:dim], shape[dim] * shape[dim + 1], *shape[dim + 2 :])


def collect(array, axis, dim):
    tiles = sent_to_all(array, axis)
    return joined_along(tiles, dim)


def merge_rows(frozen_base_rows, down_stack, up_stack, adapter_slot):
    down_rows = lax.dynamic_index_in_dim(down_stack, adapter_slot, 0, keepdims=False)
    up_projection_rows = lax.dynamic_index_in_dim(up_stack, adapter_slot, 0, keepdims=False)
    low_rank_delta = jnp.dot(down_rows, up_projection_rows, preferred_element_type=jnp.float32)
    return (frozen_base_rows.astype(jnp.float32) + low_rank_scale * low_rank_delta).astype(
        jnp.bfloat16
    )


def normalize(states, norm_gain):
    widened = states.astype(jnp.float32)
    squared_average = jnp.mean(widened * widened, axis=-1, keepdims=True)
    return (widened * lax.rsqrt(squared_average + epsilon) * norm_gain).astype(jnp.bfloat16)


def rotate(vectors, positions):
    head_dim = vectors.shape[-1]
    half_dim = head_dim // 2
    frequency = rope_theta ** (-2.0 * jnp.arange(half_dim, dtype=jnp.float32) / head_dim)
    rotation_phases = positions[:, :, None] * frequency[None, None, :]
    cosine_table = jnp.concatenate((jnp.cos(rotation_phases), jnp.cos(rotation_phases)), -1)[
        :, :, None, :
    ]
    sine_table = jnp.concatenate((jnp.sin(rotation_phases), jnp.sin(rotation_phases)), -1)[
        :, :, None, :
    ]
    turned = jnp.concatenate((-vectors[..., half_dim:], vectors[..., :half_dim]), -1)
    return vectors * cosine_table + turned * sine_table


def attend(queries, keys_new, values_new, cache_k, cache_v, lengths):
    seq_count, step_count, head_count, head_dim = queries.shape
    kv_count = keys_new.shape[2]
    grouped = queries.reshape(seq_count, step_count, kv_count, head_count // kv_count, head_dim)
    score_scale = head_dim ** (-0.5)
    old_scores = (
        jnp.einsum("bskgd,blkd->bskgl", grouped, cache_k, preferred_element_type=jnp.float32)
        * score_scale
    )
    new_scores = (
        jnp.einsum("bskgd,btkd->bskgt", grouped, keys_new, preferred_element_type=jnp.float32)
        * score_scale
    )
    live_slots = jnp.arange(cache_k.shape[1], dtype=jnp.int32)[None, :] < lengths[:, None]
    old_scores = jnp.where(live_slots[:, None, None, None, :], old_scores, -1e30)
    causal = jnp.arange(step_count)[:, None] >= jnp.arange(step_count)[None, :]
    new_scores = jnp.where(causal[None, :, None, None, :], new_scores, -1e30)
    highest = jnp.maximum(jnp.max(old_scores, -1), jnp.max(new_scores, -1))[..., None]
    old_exp = jnp.exp(old_scores - highest)
    new_exp = jnp.exp(new_scores - highest)
    denominator = jnp.sum(old_exp, -1, keepdims=True) + jnp.sum(new_exp, -1, keepdims=True)
    old_weights = (old_exp / denominator).astype(jnp.bfloat16)
    new_weights = (new_exp / denominator).astype(jnp.bfloat16)
    mixture = jnp.einsum(
        "bskgl,blkd->bskgd", old_weights, cache_v, preferred_element_type=jnp.float32
    )
    mixture = mixture + jnp.einsum(
        "bskgt,btkd->bskgd", new_weights, values_new, preferred_element_type=jnp.float32
    )
    return mixture.astype(jnp.bfloat16).reshape(seq_count, step_count, head_count * head_dim)


def local(
    states,
    norm_gain,
    query_base,
    key_base,
    value_base,
    output_base,
    query_down,
    query_up,
    key_down,
    key_up,
    value_down,
    value_up,
    output_down,
    output_up,
    adapter_layer,
    kv_lengths,
    cache_keys,
    cache_values,
):
    adapter_slot = adapter_layer[0]
    tp_size = lax.axis_size("tp")
    row_count = query_base.shape[0]
    merged_query = merge_rows(query_base, query_down, query_up, adapter_slot)
    merged_key = merge_rows(key_base, key_down, key_up, adapter_slot)
    merged_value = merge_rows(value_base, value_down, value_up, adapter_slot)
    merged_output = merge_rows(output_base, output_down, output_up, adapter_slot)
    joined = jnp.concatenate(
        (
            merged_query.reshape(row_count, tp_size, -1),
            merged_key.reshape(row_count, tp_size, -1),
            merged_value.reshape(row_count, tp_size, -1),
        ),
        2,
    ).reshape(row_count, -1)
    input_slice, output_slice = (
        lax.all_to_all(joined, "tp", split_axis=1, concat_axis=0, tiled=True),
        lax.all_to_all(merged_output, "tp", split_axis=1, concat_axis=0, tiled=True),
    )
    seq_count, step_count, model_width = states.shape
    normed = normalize(states, norm_gain)
    head_cols = HQ * DH // tp_size
    kv_cols = KVH * DH // tp_size
    flat_rows = normed.reshape(seq_count * step_count, model_width)
    columns = flat_rows
    projected = jnp.dot(
        columns,
        lax.all_gather(input_slice, "fsdp", axis=0, tiled=True),
        preferred_element_type=jnp.float32,
    )
    projected = projected.reshape(seq_count, step_count, -1)
    positions = (
        kv_lengths.astype(jnp.float32)[:, None] + jnp.arange(step_count, dtype=jnp.float32)[None, :]
    )
    queries = rotate(
        projected[:, :, :head_cols].reshape(seq_count, step_count, -1, DH), positions
    ).astype(jnp.bfloat16)
    keys_new = rotate(
        projected[:, :, head_cols : head_cols + kv_cols].reshape(seq_count, step_count, -1, DH),
        positions,
    ).astype(jnp.bfloat16)
    values_new = (
        projected[:, :, head_cols + kv_cols :]
        .reshape(seq_count, step_count, -1, DH)
        .astype(jnp.bfloat16)
    )
    attended = attend(queries, keys_new, values_new, cache_keys, cache_values, kv_lengths)
    all_heads = collect(attended, "tp", 2)
    flat_heads = all_heads.reshape(seq_count * step_count, -1)
    columns = flat_heads
    low_rank_delta = jnp.dot(
        columns,
        lax.all_gather(output_slice, "fsdp", axis=0, tiled=True),
        preferred_element_type=jnp.float32,
    )
    low_rank_delta = low_rank_delta.reshape(seq_count, step_count, -1)
    return low_rank_delta.astype(jnp.bfloat16)


def solution(mesh):
    in_specs = (
        P("fsdp", None, None),
        P(),
        P(("fsdp", "tp"), None),
        P(("fsdp", "tp"), None),
        P(("fsdp", "tp"), None),
        P(("fsdp", "tp"), None),
        P(None, ("fsdp", "tp"), None),
        P(),
        P(None, ("fsdp", "tp"), None),
        P(),
        P(None, ("fsdp", "tp"), None),
        P(),
        P(None, ("fsdp", "tp"), None),
        P(),
        P(),
        P("fsdp"),
        P("fsdp", None, "tp", None),
        P("fsdp", None, "tp", None),
    )
    out_specs = P("fsdp", None, "tp")
    return jax.shard_map(local, mesh=mesh, in_specs=in_specs, out_specs=out_specs, check_vma=False)
```

profile of v0, /device:TPU:1, one launch (start us, length us, event | category | flops | bytes accessed | tf_op | source)
XLA Modules:
  0.0 290.6 jit_solution(4913275454677924409)
XLA Ops:
  7.3 2.0 fusion.7
  9.3 0.1 copy.110
  9.4 0.9 fusion.33
  10.3 1.1 fusion.34
  11.5 0.1 pad_maximum_fusion
  11.6 26.0 %all_to_all.40 = bf16[64,8,1280]{2,0,1:T(8,128)(2,1)} all-to-all(bf16[64,8,1280]{2,0,1:T(8,128)(2,1)S(1)} %pad_maximum_fusion), channel_id=1, replica_groups=mesh['fsdp'=16,'tp'=8] {'tp'}, dimensions={1} | all-to-all | bytes 2621440 | tf_op jit(solution)/shard_map/all_to_all | solution.py:130
  37.7 1.7 fusion.6
  39.3 0.1 copy.109
  39.4 21.3 %all_to_all.41 = bf16[64,8,1024]{2,0,1:T(8,128)(2,1)} all-to-all(bf16[64,8,1024]{2,0,1:T(8,128)(2,1)S(1)} %bitcast.136), channel_id=1, replica_groups=mesh['fsdp'=16,'tp'=8] {'tp'}, dimensions={1} | all-to-all | bytes 2097152 | tf_op jit(solution)/shard_map/all_to_all | solution.py:131
  60.9 1.2 fusion.8
  62.1 0.3 multiply_cosine_fusion
  62.5 1.5 fusion.10
  63.9 92.0 %all-gather.3.cloned.1.call-done = bf16[8192,1280]{1,0:T(8,128)(2,1)} async-done(((bf16[512,1280]{1,0:T(8,128)(2,1)}), bf16[8192,1280]{1,0:T(8,128)(2,1)}) %all-gather.3.cloned.1.call-update) | async-done | bytes 20971536 | tf_op jit(solution)/shard_map/all_gather | solution.py:141
  155.9 11.4 %fusion = f32[32,4,1280]{2,0,1:T(8,128)S(1)} fusion(bf16[8192,1280]{1,0:T(8,128)(2,1)} %all-gather.3.cloned.1.call-done, bf16[32,4,8192]{2,1,0:T(4,128)(2,1)S(1)} %fusion.10), kind=kOutput, calls=%fused_computation | convolution fusion | flops 2684354560 | bytes 23724032 | tf_op jit(solution)/shard_map/dot_general | solution.py:139
  167.4 0.1 fusion.54
  167.7 0.1 copy.92
  167.8 0.2 slice_negate_fusion
  168.0 0.2 fusion.43
  168.2 1.3 fusion.71
  169.5 0.4 copy-done.4
  170.0 1.6 fusion.70
  171.5 0.3 fusion.44
  171.8 0.8 fusion.17
  172.6 0.8 fusion.20
  173.5 0.4 fusion.27
  173.9 0.1 copy.75
  174.0 0.3 broadcast_in_dim.26
  174.3 57.7 %all_to_all.42 = bf16[8,32,4,1024]{3,1,2,0:T(8,128)(2,1)S(1)} all-to-all(bf16[8,32,4,1024]{3,1,2,0:T(8,128)(2,1)S(1)} %broadcast_in_dim.26), channel_id=1, replica_groups=mesh['fsdp'=16,'tp'=8] {'tp'}, dimensions={0} | all-to-all | bytes 4194304 | tf_op jit(solution)/shard_map/all_to_all | solution.py:18
  232.0 0.2 copy.91
  232.1 42.5 %all-gather.5.cloned.1.call-done = bf16[8192,1024]{1,0:T(8,128)(2,1)} async-done(((bf16[512,1024]{1,0:T(8,128)(2,1)}), bf16[8192,1024]{1,0:T(8,128)(2,1)}) %all-gather.5.cloned.1.call-update) | async-done | bytes 16777232 | tf_op jit(solution)/shard_map/all_gather | solution.py:166
  274.6 8.2 %fusion.24 = bf16[32,4,1024]{2,0,1:T(8,128)(2,1)S(1)} fusion(bf16[32,4,8192]{2,0,1:T(8,128)(2,1)S(1)} %bitcast.128, bf16[8192,1024]{1,0:T(8,128)(2,1)} %all-gather.5.cloned.1.call-done), kind=kOutput, calls=%fused_computation.29 | convolution fusion | flops 2147614720 | bytes 19136512 | tf_op jit(solution)/shard_map/dot_general | solution.py:164
  282.8 0.9 copy.78
  (41 shorter events, 0.6 us)
Async XLA Ops:
  6.5 2.9 copy-start
  6.5 149.4 %all-gather.3.cloned.1.call-start = ((), (), s32[]{:S(2)}) async-start(), calls=%async_computation.3 | async-start | bytes 22282240 | tf_op jit(solution)/shard_map/all_gather | solution.py:141
  7.3 2.1 copy-start.6
  7.3 3.0 %copy-start.7 = (bf16[64,1024]{1,0:T(8,128)(2,1)S(1)}, bf16[64,1024]{1,0:T(8,128)(2,1)}, u32[]{:S(2)}) copy-start(bf16[64,1024]{1,0:T(8,128)(2,1)} %param.21) | copy-start | bytes 393220
  11.6 26.0 %copy-start.5 = (bf16[64,8192]{1,0:T(8,128)(2,1)S(1)}, bf16[64,8192]{1,0:T(8,128)(2,1)}, u32[]{:S(2)}) copy-start(bf16[64,8192]{1,0:T(8,128)(2,1)} %param.23) | copy-start | bytes 3145732
  37.6 237.0 %all-gather.5.cloned.1.call-start = ((), (), s32[]{:S(2)}) async-start(), calls=%async_computation.4 | async-start | bytes 17825792 | tf_op jit(solution)/shard_map/all_gather | solution.py:166
  39.4 21.3 %copy-start.9 = (s32[32]{0:T(128)S(1)}, s32[32]{0:T(128)}, u32[]{:S(2)}) copy-start(s32[32]{0:T(128)} %param.33) | copy-start | bytes 388
  39.4 21.5 %copy-start.2 = (bf16[32,4,8192]{2,1,0:T(4,128)(2,1)S(1)}, bf16[32,4,8192]{2,1,0:T(4,128)(2,1)}, u32[]{:S(2)}) copy-start(bf16[32,4,8192]{2,1,0:T(4,128)(2,1)} %param.18) | copy-start | bytes 6291460
  60.7 1.7 copy-start.8
  60.8 1.7 copy-start.3
  167.8 2.2 copy-start.4
  170.0 2.7 copy-start.10
  274.6 9.1 %copy-start.1 = (bf16[4,64,1024]{2,1,0:T(8,128)(2,1)S(1)}, bf16[4,64,1024]{2,1,0:T(8,128)(2,1)}, u32[]{:S(2)}) copy-start(bf16[4,64,1024]{2,1,0:T(8,128)(2,1)} %param.29) | copy-start | bytes 1572868
Sparse Core Ops, SparseCore 0:
  37.7 118.1 all-gather.2
  157.6 116.9 all-gather.4
where the time goes:
time: 291 us
  waiting for transfers between devices  135 us (46%)
  blocking collectives  105 us (36%)
  matrix products  29.2 us (10%)
  between operations  14.5 us (5%)
  other arithmetic  4.89 us (2%)
    all_gather x1, waiting for transfers between devices, local(): lax.all_gather(input_slice, 'fsdp', axis=0, tiled=True)  92 us
    all_to_all x1, blocking collectives, sent_to_all(): return lax.all_to_all(copies, axis, split_axis=0, concat_axis=0, tiled=True)  57.7 us
    all_gather x1, waiting for transfers between devices, local(): lax.all_gather(output_slice, 'fsdp', axis=0, tiled=True)  42.5 us
    all_to_all x1, blocking collectives, local(): lax.all_to_all(joined, 'tp', split_axis=1, concat_axis=0, tiled=True)  26 us
    all_to_all x1, blocking collectives, local(): lax.all_to_all(merged_output, 'tp', split_axis=1, concat_axis=0, tiled=True)  21.3 us
    dot_general x1, matrix products, local(): jnp.dot(columns, lax.all_gather(input_slice, 'fsdp', axis=0, tiled=True),...  11.4 us
    dot_general x1, matrix products, local(): jnp.dot(columns, lax.all_gather(output_slice, 'fsdp', axis=0, tiled=True)...  8.16 us
  transfers between devices with their start and end apart: 2, of which 2 were waited for; matrix products, arithmetic and copies ran while one was open for 8% of the time, Pallas kernels for 0%

commit v1 on v0

--- a/solution.py
+++ b/solution.py
@@ -1,32 +1,367 @@
+import functools
+
 import jax
 import jax.numpy as jnp
 from jax import lax
+from jax.experimental import pallas as pl
+from jax.experimental.pallas import tpu as pltpu
 from jax.sharding import PartitionSpec as P
 
 HQ = 64
 KVH = 8
 DH = 128
-
+MESH = pl.DeviceIdType.MESH
 
 rope_theta = 1000000.0
 low_rank_scale = 0.5
 epsilon = 1e-06
 
-
-def sent_to_all(array, axis):
-    copies = jnp.broadcast_to(array, (lax.axis_size(axis), *array.shape))
-    return lax.all_to_all(copies, axis, split_axis=0, concat_axis=0, tiled=True)
-
-
-def joined_along(tiles, dim):
-    tiles = jnp.moveaxis(tiles, 0, dim)
-    shape = tiles.shape
-    return tiles.reshape(*shape[:dim], shape[dim] * shape[dim + 1], *shape[dim + 2 :])
-
-
-def collect(array, axis, dim):
-    tiles = sent_to_all(array, axis)
-    return joined_along(tiles, dim)
+TOK = 128
+WROWS = 64
+PLANE = 2048
+QKV = 1280
+OUT = 1024
+CW = 256
+NC = QKV // CW
+NO = OUT // CW
+
+
+def coords():
+    f = lax.axis_index("fsdp")
+    t = lax.axis_index("tp")
+    return f // 4, lax.rem(f // 2, 2), lax.rem(f, 2), t
+
+
+def flip(v, bit):
+    return 1 - v if bit else v
+
+
+def xor_z(z, e):
+    hi, lo = z // 2, lax.rem(z, 2)
+    return flip(hi, e >> 1) * 2 + flip(lo, e & 1)
+
+
+def xor_t(t, d):
+    b2, b1, b0 = t // 4, lax.rem(t // 2, 2), lax.rem(t, 2)
+    return flip(b2, (d >> 2) & 1) * 4 + flip(b1, (d >> 1) & 1) * 2 + flip(b0, d & 1)
+
+
+def dev(z, xl, c, t):
+    return ((z * 2 + xl) * 2 + c, t)
+
+
+def remote(src, dst, ssem, rsem, device):
+    return pltpu.make_async_remote_copy(
+        src_ref=src, dst_ref=dst, send_sem=ssem, recv_sem=rsem, device_id=device, device_id_type=MESH
+    )
+
+
+def project_kernel(
+    a_ref, w_ref, o_ref, out_ref, wo_ref,
+    abuf, wbuf, acc, crecv,
+    a_ss, a_rs, w1_ss, w1_rs, w2_ss, w2_rs, w3_ss, w3_rs, c_ss, c_rs,
+):
+    z, xl, c, t = coords()
+    xh = t // 4
+    y4 = xh * 4
+    xpart = dev(z, 1 - xl, c, t)
+    cpart = dev(z, xl, 1 - c, t)
+
+    def plane_peer(d):
+        return dev(z, flip(xl, d >> 2), c, xor_t(t, d))
+
+    def z_peer(e):
+        return dev(xor_z(z, e), xl, c, t)
+
+    barrier = pltpu.get_barrier_semaphore()
+    peers = [plane_peer(d) for d in range(1, 8)] + [z_peer(e) for e in range(1, 4)] + [xpart, cpart]
+    for p in peers:
+        pl.semaphore_signal(barrier, inc=1, device_id=p, device_id_type=MESH)
+    pl.semaphore_wait(barrier, len(peers))
+
+    def a_copy(e):
+        cols = pl.ds(pl.multiple_of(xor_z(z, e) * PLANE, PLANE), PLANE)
+        if e == 0:
+            return pltpu.make_async_copy(a_ref.at[:, cols], abuf.at[0], a_rs.at[0])
+        return remote(a_ref.at[:, cols], abuf.at[e], a_ss.at[e], a_rs.at[e], z_peer(e))
+
+    my_slot = (xl * 2 + c) * 8 + t
+
+    def w1_copy(ch, d):
+        td = xor_t(t, d)
+        cols = pl.ds(pl.multiple_of(td * QKV + ch * CW, CW), CW)
+        src = w_ref.at[:, cols]
+        dst = wbuf.at[ch, my_slot]
+        if d == 0:
+            return pltpu.make_async_copy(src, dst, w1_rs.at[ch, 0])
+        return remote(src, dst, w1_ss.at[ch, d], w1_rs.at[ch, d], plane_peer(d))
+
+    def o1_copy(d):
+        cols = pl.ds(pl.multiple_of(xor_t(t, d) * OUT, OUT), OUT)
+        src = o_ref.at[:, cols]
+        dst = wo_ref.at[my_slot]
+        if d == 0:
+            return pltpu.make_async_copy(src, dst, w1_rs.at[NC, 0])
+        return remote(src, dst, w1_ss.at[NC, d], w1_rs.at[NC, d], plane_peer(d))
+
+    def group_base(g, core):
+        lo = xl if g in (0, 3) else 1 - xl
+        hi = xh if g in (0, 2) else 1 - xh
+        return (lo * 2 + core) * 8 + hi * 4
+
+    def rows_of(k, base):
+        if k is None:
+            return wo_ref.at[pl.ds(base, 4)]
+        return wbuf.at[k, pl.ds(base, 4)]
+
+    def w2_copy(k, g):
+        i = NC if k is None else k
+        ref = rows_of(k, group_base(g, c))
+        return remote(ref, ref, w2_ss.at[i, g], w2_rs.at[i, g], xpart)
+
+    def w2_wait(k, g):
+        i = NC if k is None else k
+        ref = rows_of(k, group_base(g + 2, c))
+        remote(ref, ref, w2_ss.at[i, g], w2_rs.at[i, g], xpart).wait_recv()
+
+    def w3_copy(k, g):
+        i = NC if k is None else k
+        ref = rows_of(k, group_base(g, c))
+        return remote(ref, ref, w3_ss.at[i, g], w3_rs.at[i, g], cpart)
+
+    def w3_wait(k, g):
+        i = NC if k is None else k
+        ref = rows_of(k, group_base(g, 1 - c))
+        remote(ref, ref, w3_ss.at[i, g], w3_rs.at[i, g], cpart).wait_recv()
+
+    def c_copy(ch, e):
+        return remote(acc.at[ch, e], crecv.at[ch, e - 1], c_ss.at[ch, e], c_rs.at[ch, e], z_peer(e))
+
+    def start_w1(ch, carry):
+        for d in range(8):
+            w1_copy(ch, d).start()
+        return carry
+
+    start_w1(0, 0)
+    for e in (1, 3, 2, 0):
+        a_copy(e).start()
+    lax.fori_loop(1, NC, start_w1, 0)
+    for d in range(8):
+        o1_copy(d).start()
+
+    def gather(k, arrived):
+        for g in range(2):
+            for d in range(g * 4, g * 4 + 4):
+                arrived(d)
+            w2_copy(k, g).start()
+            w3_copy(k, g).start()
+        for g in range(2):
+            w2_wait(k, g)
+            w3_copy(k, g + 2).start()
+        for g in range(4):
+            w3_wait(k, g)
+
+    def chunk(ch, carry):
+        def arrived(d):
+            if d == 0:
+                w1_copy(ch, 0).wait()
+            else:
+                ref = wbuf.at[ch, (flip(xl, d >> 2) * 2 + c) * 8 + xor_t(t, d)]
+                remote(ref, ref, w1_ss.at[ch, d], w1_rs.at[ch, d], plane_peer(d)).wait_recv()
+
+        gather(ch, arrived)
+
+        @pl.when(ch == 0)
+        def _():
+            a_copy(0).wait()
+            for e in (1, 3, 2):
+                a_copy(e).wait_recv()
+
+        rows = abuf[...].reshape(4 * TOK, PLANE)
+        part = jnp.dot(rows, wbuf[ch].reshape(PLANE, CW), preferred_element_type=jnp.float32)
+        acc[ch] = part.reshape(4, TOK, CW)
+        for e in (1, 3, 2):
+            c_copy(ch, e).start()
+        return carry
+
+    lax.fori_loop(0, NC, chunk, 0)
+
+    def arrived_o(d):
+        if d == 0:
+            o1_copy(0).wait()
+        else:
+            ref = wo_ref.at[(flip(xl, d >> 2) * 2 + c) * 8 + xor_t(t, d)]
+            remote(ref, ref, w1_ss.at[NC, d], w1_rs.at[NC, d], plane_peer(d)).wait_recv()
+
+    gather(None, arrived_o)
+
+    for ch in range(NC):
+        for e in range(1, 4):
+            c_copy(ch, e).wait_recv()
+        out_ref[:, ch * CW : (ch + 1) * CW] = acc[ch, 0] + crecv[ch, 0] + crecv[ch, 1] + crecv[ch, 2]
+
+    for e in range(1, 4):
+        a_copy(e).wait_send()
+
+    def drain(ch, carry):
+        for d in range(1, 8):
+            w1_copy(ch, d).wait_send()
+        for g in range(2):
+            w2_copy(ch, g).wait_send()
+        for g in range(4):
+            w3_copy(ch, g).wait_send()
+        for e in range(1, 4):
+            c_copy(ch, e).wait_send()
+        return carry
+
+    lax.fori_loop(0, NC, drain, 0)
+    for d in range(1, 8):
+        o1_copy(d).wait_send()
+    for g in range(2):
+        w2_copy(None, g).wait_send()
+    for g in range(4):
+        w3_copy(None, g).wait_send()
+
+
+def output_kernel(
+    h_ref, wo_ref, out_ref,
+    abuf, wbuf, acc, crecv,
+    wl_s, a_ss, a_rs, c_ss, c_rs,
+):
+    z, xl, c, t = coords()
+    zd = t // 2
+    half = lax.rem(t, 2)
+
+    def target(d):
+        return dev(zd, xl, c, xor_t(t, d))
+
+    def z_peer(e):
+        return dev(xor_z(z, e), xl, c, t)
+
+    slot = lax.rem(z // 2 + zd // 2, 2) * 2 + lax.rem(lax.rem(z, 2) + lax.rem(zd, 2), 2)
+    here = z == zd
+
+    def source(e, h):
+        return dev(xor_z(z, e), xl, c, 2 * z + h)
+
+    loads = [
+        pltpu.make_async_copy(wo_ref, wbuf, wl_s.at[0]),
+    ]
+    for load in loads:
+        load.start()
+
+    barrier = pltpu.get_barrier_semaphore()
+    count = 0
+    for e in range(1, 4):
+        pl.semaphore_signal(barrier, inc=1, device_id=z_peer(e), device_id_type=MESH)
+    for d in range(8):
+        pl.semaphore_signal(barrier, inc=1, device_id=target(d), device_id_type=MESH)
+    for e in range(4):
+        for h in range(2):
+            pl.semaphore_signal(barrier, inc=1, device_id=source(e, h), device_id_type=MESH)
+    pl.semaphore_wait(barrier, 3 + 8 + 8)
+
+    def a_send(d):
+        dst = abuf.at[slot, :, pl.ds(pl.multiple_of(half * OUT, OUT), OUT)]
+        return remote(h_ref, dst, a_ss.at[d], a_rs.at[slot, half], target(d))
+
+    def a_local():
+        dst = abuf.at[0, :, pl.ds(pl.multiple_of(half * OUT, OUT), OUT)]
+        return pltpu.make_async_copy(h_ref, dst, a_rs.at[0, half])
+
+    @pl.when(here)
+    def _():
+        a_local().start()
+
+    @pl.when(jnp.logical_not(here))
+    def _():
+        a_send(0).start()
+
+    for d in range(1, 8):
+        a_send(d).start()
+
+    for e in range(4):
+        for h in range(2):
+            ref = abuf.at[e, :, pl.ds(h * OUT, OUT)]
+            pltpu.make_async_copy(ref, ref, a_rs.at[e, h]).wait()
+    for load in loads:
+        load.wait()
+
+    def c_copy(ch, e):
+        return remote(acc.at[ch, e], crecv.at[ch, e - 1], c_ss.at[ch, e], c_rs.at[ch, e], z_peer(e))
+
+    own = []
+    for ch in range(NO):
+        w = wbuf[:, :, ch * CW : (ch + 1) * CW].reshape(PLANE, CW)
+        part = jnp.dot(abuf[...].reshape(4 * TOK, PLANE), w, preferred_element_type=jnp.float32)
+        acc[ch] = part.reshape(4, TOK, CW)
+        for e in (1, 3, 2):
+            c_copy(ch, e).start()
+    for ch in range(NO):
+        for e in range(1, 4):
+            c_copy(ch, e).wait_recv()
+        total = acc[ch, 0] + crecv[ch, 0] + crecv[ch, 1] + crecv[ch, 2]
+        out_ref[:, ch * CW : (ch + 1) * CW] = total.astype(jnp.bfloat16)
+
+    @pl.when(jnp.logical_not(here))
+    def _():
+        a_send(0).wait_send()
+
+    for d in range(1, 8):
+        a_send(d).wait_send()
+    for ch in range(NO):
+        for e in range(1, 4):
+            c_copy(ch, e).wait_send()
+
+
+VM = pl.BlockSpec(memory_space=pltpu.VMEM)
+ANY = pl.BlockSpec(memory_space=pl.ANY)
+DMA = pltpu.SemaphoreType.DMA
+
+
+def project(normed, joined, merged_output):
+    return pl.pallas_call(
+        project_kernel,
+        out_shape=(
+            jax.ShapeDtypeStruct((TOK, QKV), jnp.float32),
+            jax.ShapeDtypeStruct((32, WROWS, OUT), jnp.bfloat16),
+        ),
+        in_specs=[VM, VM, ANY],
+        out_specs=(VM, ANY),
+        scratch_shapes=[
+            pltpu.VMEM((4, TOK, PLANE), jnp.bfloat16),
+            pltpu.VMEM((NC, 32, WROWS, CW), jnp.bfloat16),
+            pltpu.VMEM((NC, 4, TOK, CW), jnp.float32),
+            pltpu.VMEM((NC, 3, TOK, CW), jnp.float32),
+            DMA((4,)), DMA((4,)),
+            DMA((NC + 1, 8)), DMA((NC + 1, 8)),
+            DMA((NC + 1, 2)), DMA((NC + 1, 2)),
+            DMA((NC + 1, 4)), DMA((NC + 1, 4)),
+            DMA((NC, 4)), DMA((NC, 4)),
+        ],
+        compiler_params=pltpu.CompilerParams(collective_id=0, has_side_effects=True, vmem_limit_bytes=48 << 20),
+        name="project",
+    )(normed, joined, merged_output)
+
+
+def output_projection(heads, weights):
+    return pl.pallas_call(
+        output_kernel,
+        out_shape=jax.ShapeDtypeStruct((TOK, OUT), jnp.bfloat16),
+        in_specs=[VM, ANY],
+        out_specs=VM,
+        scratch_shapes=[
+            pltpu.VMEM((4, TOK, PLANE), jnp.bfloat16),
+            pltpu.VMEM((32, WROWS, OUT), jnp.bfloat16),
+            pltpu.VMEM((NO, 4, TOK, CW), jnp.float32),
+            pltpu.VMEM((NO, 3, TOK, CW), jnp.float32),
+            DMA((1,)),
+            DMA((8,)), DMA((4, 2)),
+            DMA((NO, 4)), DMA((NO, 4)),
+        ],
+        compiler_params=pltpu.CompilerParams(collective_id=1, has_side_effects=True, vmem_limit_bytes=48 << 20),
+        name="output_projection",
+    )(heads, weights)
 
 
 def merge_rows(frozen_base_rows, down_stack, up_stack, adapter_slot):
@@ -126,21 +461,11 @@
         ),
         2,
     ).reshape(row_count, -1)
-    input_slice, output_slice = (
-        lax.all_to_all(joined, "tp", split_axis=1, concat_axis=0, tiled=True),
-        lax.all_to_all(merged_output, "tp", split_axis=1, concat_axis=0, tiled=True),
-    )
     seq_count, step_count, model_width = states.shape
-    normed = normalize(states, norm_gain)
+    normed = normalize(states, norm_gain).reshape(seq_count * step_count, model_width)
+    projected, output_rows = project(normed, joined, merged_output)
     head_cols = HQ * DH // tp_size
     kv_cols = KVH * DH // tp_size
-    flat_rows = normed.reshape(seq_count * step_count, model_width)
-    columns = flat_rows
-    projected = jnp.dot(
-        columns,
-        lax.all_gather(input_slice, "fsdp", axis=0, tiled=True),
-        preferred_element_type=jnp.float32,
-    )
     projected = projected.reshape(seq_count, step_count, -1)
     positions = (
         kv_lengths.astype(jnp.float32)[:, None] + jnp.arange(step_count, dtype=jnp.float32)[None, :]
@@ -158,16 +483,8 @@
         .astype(jnp.bfloat16)
     )
     attended = attend(queries, keys_new, values_new, cache_keys, cache_values, kv_lengths)
-    all_heads = collect(attended, "tp", 2)
-    flat_heads = all_heads.reshape(seq_count * step_count, -1)
-    columns = flat_heads
-    low_rank_delta = jnp.dot(
-        columns,
-        lax.all_gather(output_slice, "fsdp", axis=0, tiled=True),
-        preferred_element_type=jnp.float32,
-    )
-    low_rank_delta = low_rank_delta.reshape(seq_count, step_count, -1)
-    return low_rank_delta.astype(jnp.bfloat16)
+    update = output_projection(attended.reshape(seq_count * step_count, -1), output_rows)
+    return update.reshape(seq_count, step_count, -1)
 
 
 def solution(mesh):

time: 291 us -> 201 us (0.69)
  the two profiles are of different devices: /device:TPU:1 before, /device:TPU:32 now
where the time goes in v1:
time: 201 us; the launch traced here: 200 us
  Pallas kernels  173 us (86%)
  matrix products  10.9 us (5%)
  local copies, waits for them, and re-layouts  9.4 us (5%)
  other arithmetic  6.34 us (3%)
    pallas_call x1, Pallas kernels, project(): pl.pallas_call(project_kernel, out_shape=(jax.ShapeDtypeStruct((TOK, QKV)...  95 us
    pallas_call x1, Pallas kernels, output_projection(): pl.pallas_call(output_kernel, out_shape=jax.ShapeDtypeStruct((TOK, OUT),...  77.5 us
    dot_general x4, matrix products, merge_rows(): jnp.dot(down_rows, up_projection_rows, preferred_element_type=jnp.float32)  6.81 us
    unnamed x29, local copies, waits for them, and re-layouts  5.59 us

profile of v1, /device:TPU:32, one launch (start us, length us, event | category | flops | bytes accessed | tf_op | source)
XLA Modules:
  0.0 200.2 jit_solution(16986225418730043548)
XLA Ops:
  0.7 2.0 %fusion.3 = bf16[64,8192]{1,0:T(8,128)(2,1)S(1)} fusion(bf16[64,8192]{1,0:T(8,128)(2,1)} %param.20, bf16[4,64,8192]{2,1,0:T(8,128)(2,1)} %param.25, s32[]{:T(128)S(6)} %select_n.24, bf16[4,64,64]{2,1,0:T(8,128)(2,1)} %param.24), kind=kOutput, calls=%fused_computation.5 | convolution fusion | flops 69206016 | bytes 3163136 | tf_op jit(solution)/shard_map/dot_general | solution.py:370
  2.8 0.6 copy.26
  3.4 0.9 fusion.25
  4.3 1.1 fusion.24
  5.5 0.1 pad_maximum_fusion
  5.6 1.3 copy.29
  6.9 2.8 %fusion.2.o_ref = bf16[64,8192]{1,0:T(8,128)(2,1)} fusion(bf16[64,8192]{1,0:T(8,128)(2,1)S(1)} %copy-done.6, bf16[4,64,8192]{2,1,0:T(8,128)(2,1)} %param.31, s32[]{:T(128)S(6)} %select_n.24, bf16[4,64,64]{2,1,0:T(8,128)(2,1)} %param.30), kind=kOutput, calls=%fused_computation.4 | convolution fusion | flops 69206016 | bytes 3163136 | tf_op jit(solution)/shard_map/dot_general | solution.py:370
  9.7 1.2 fusion.4
  10.9 2.6 %fusion.6 = bf16[32,4,8192]{2,1,0:T(4,128)(2,1)} fusion(bf16[32,4,8192]{2,1,0:T(4,128)(2,1)S(1)} %copy-done.4, f32[8192]{0:T(1024)S(1)} %copy-done.9, f32[32,4]{1,0:T(8,128)S(1)} %add_rsqrt_fusion), kind=kLoop, calls=%fused_computation.10 | loop fusion | flops 4194304 | bytes 4227584 | tf_op jit(solution)/shard_map/convert_element_type | solution.py:379
  13.5 2.5 %reshape.181.a_ref = bf16[128,8192]{1,0:T(8,128)(2,1)S(1)} reshape(bf16[32,4,8192]{2,1,0:T(4,128)(2,1)} %fusion.6) | data formatting | bytes 4194304 | tf_op jit(solution)/shard_map/reshape | solution.py:465
  16.0 1.3 copy-done.1
  17.3 1.2 copy-done.2
  18.6 95.0 %project.1 = (f32[128,1280]{1,0:T(8,128)S(1)}, bf16[32,64,1024]{2,1,0:T(8,128)(2,1)}) custom-call(bf16[128,8192]{1,0:T(8,128)(2,1)S(1)} %reshape.181.a_ref, bf16[64,10240]{1,0:T(8,128)(2,1)S(1)} %bitcast.107, bf16[64,8192]{1,0:T(8,128)(2,1)S(1)} %copy-done.2), custom_call_target="tpu_custom_call" | custom-call | tf_op jit(solution)/shard_map/project/pallas_call | solution.py:323
  113.5 0.2 reshape.186
  113.8 0.2 reshape.187
  114.0 0.2 slice_negate_fusion
  114.3 0.1 copy-done.10
  114.4 0.1 iota_add_fusion
  114.5 0.5 multiply_cosine_fusion
  115.0 0.1 pad_maximum_fusion.1
  115.2 0.2 fusion.34
  115.4 0.1 fusion.42
  115.5 1.3 fusion.63
  116.9 0.1 iota_compare_fusion
  117.0 1.6 fusion.62
  118.5 0.3 fusion.35
  118.8 0.8 fusion.12
  119.6 0.9 fusion.15
  120.5 0.4 fusion.18
  120.9 0.9 copy-done.3
  121.8 77.5 %output_projection.1 = bf16[128,1024]{1,0:T(8,128)(2,1)S(1)} custom-call(bf16[128,1024]{1,0:T(8,128)(2,1)S(1)} %bitcast.108, bf16[32,64,1024]{2,1,0:T(8,128)(2,1)S(1)} %copy-done.3), custom_call_target="tpu_custom_call" | custom-call | tf_op jit(solution)/shard_map/output_projection/pallas_call | solution.py:348
  199.4 0.8 reshape.193
  (31 shorter events, 0.3 us)
Async XLA Ops:
  0.0 3.4 %copy-start = (bf16[4,64,1024]{2,1,0:T(8,128)(2,1)S(1)}, bf16[4,64,1024]{2,1,0:T(8,128)(2,1)}, u32[]{:S(2)}) copy-start(bf16[4,64,1024]{2,1,0:T(8,128)(2,1)} %param.27) | copy-start | bytes 1572868
  0.7 2.7 %copy-start.7 = (bf16[64,1024]{1,0:T(8,128)(2,1)S(1)}, bf16[64,1024]{1,0:T(8,128)(2,1)}, u32[]{:S(2)}) copy-start(bf16[64,1024]{1,0:T(8,128)(2,1)} %param.21) | copy-start | bytes 393220
  2.7 1.6 copy-start.8
  5.5 1.4 copy-start.6
  6.9 2.8 %copy-start.4 = (bf16[32,4,8192]{2,1,0:T(4,128)(2,1)S(1)}, bf16[32,4,8192]{2,1,0:T(4,128)(2,1)}, u32[]{:S(2)}) copy-start(bf16[32,4,8192]{2,1,0:T(4,128)(2,1)} %param.18) | copy-start | bytes 6291460
  6.9 4.0 %copy-start.9 = (f32[8192]{0:T(1024)S(1)}, f32[8192]{0:T(1024)}, u32[]{:S(2)}) copy-start(f32[8192]{0:T(1024)} %param.19) | copy-start | bytes 98308
  16.0 1.3 copy-start.1
  17.3 1.2 copy-start.2
  113.7 0.7 copy-start.10
  114.0 2.9 %copy-start.5 = (bf16[32,512,1,128]{3,1,2,0:T(8,128)(2,1)S(1)}, bf16[32,512,1,128]{3,1,2,0:T(8,128)(2,1)}, u32[]{:S(2)}) copy-start(bf16[32,512,1,128]{3,1,2,0:T(8,128)(2,1)} %param.34) | copy-start | bytes 12582916
  116.9 2.7 %copy-start.11 = (bf16[32,512,1,128]{3,1,2,0:T(8,128)(2,1)S(1)}, bf16[32,512,1,128]{3,1,2,0:T(8,128)(2,1)}, u32[]{:S(2)}) copy-start(bf16[32,512,1,128]{3,1,2,0:T(8,128)(2,1)} %param.35) | copy-start | bytes 12582916
  119.6 2.2 %copy-start.3 = (bf16[32,64,1024]{2,1,0:T(8,128)(2,1)S(1)}, bf16[32,64,1024]{2,1,0:T(8,128)(2,1)}, u32[]{:S(2)}) copy-start(bf16[32,64,1024]{2,1,0:T(8,128)(2,1)} %get-tuple-element.8.wo_ref) | copy-start | bytes 12582916

commit v2 on v1

--- a/solution.py
+++ b/solution.py
@@ -149,51 +149,53 @@
     for d in range(8):
         o1_copy(d).start()
 
-    def gather(k, arrived):
+    def relay(k):
         for g in range(2):
             for d in range(g * 4, g * 4 + 4):
-                arrived(d)
+                source_slot = (flip(xl, d >> 2) * 2 + c) * 8 + xor_t(t, d)
+                if d == 0:
+                    (o1_copy(0) if k is None else w1_copy(k, 0)).wait()
+                elif k is None:
+                    ref = wo_ref.at[source_slot]
+                    remote(ref, ref, w1_ss.at[NC, d], w1_rs.at[NC, d], plane_peer(d)).wait_recv()
+                else:
+                    ref = wbuf.at[k, source_slot]
+                    remote(ref, ref, w1_ss.at[k, d], w1_rs.at[k, d], plane_peer(d)).wait_recv()
             w2_copy(k, g).start()
             w3_copy(k, g).start()
+
+    def share(k):
         for g in range(2):
             w2_wait(k, g)
             w3_copy(k, g + 2).start()
+
+    def multiply(ch):
         for g in range(4):
-            w3_wait(k, g)
-
-    def chunk(ch, carry):
-        def arrived(d):
-            if d == 0:
-                w1_copy(ch, 0).wait()
-            else:
-                ref = wbuf.at[ch, (flip(xl, d >> 2) * 2 + c) * 8 + xor_t(t, d)]
-                remote(ref, ref, w1_ss.at[ch, d], w1_rs.at[ch, d], plane_peer(d)).wait_recv()
-
-        gather(ch, arrived)
-
-        @pl.when(ch == 0)
-        def _():
-            a_copy(0).wait()
-            for e in (1, 3, 2):
-                a_copy(e).wait_recv()
-
+            w3_wait(ch, g)
         rows = abuf[...].reshape(4 * TOK, PLANE)
         part = jnp.dot(rows, wbuf[ch].reshape(PLANE, CW), preferred_element_type=jnp.float32)
         acc[ch] = part.reshape(4, TOK, CW)
         for e in (1, 3, 2):
             c_copy(ch, e).start()
-        return carry
-
-    lax.fori_loop(0, NC, chunk, 0)
-
-    def arrived_o(d):
-        if d == 0:
-            o1_copy(0).wait()
-        else:
-            ref = wo_ref.at[(flip(xl, d >> 2) * 2 + c) * 8 + xor_t(t, d)]
-            remote(ref, ref, w1_ss.at[NC, d], w1_rs.at[NC, d], plane_peer(d)).wait_recv()
-
-    gather(None, arrived_o)
+
+    relay(0)
+    for ch in range(3):
+        relay(ch + 1)
+        share(ch)
+    a_copy(0).wait()
+    for e in (1, 3, 2):
+        a_copy(e).wait_recv()
+    multiply(0)
+    relay(4)
+    share(3)
+    multiply(1)
+    relay(None)
+    share(4)
+    for ch in range(2, NC):
+        multiply(ch)
+    share(None)
+    for g in range(4):
+        w3_wait(None, g)
 
     for ch in range(NC):
         for e in range(1, 4):
@@ -225,7 +227,7 @@
 
 def output_kernel(
     h_ref, wo_ref, out_ref,
-    abuf, wbuf, acc, crecv,
+    abuf, wbuf, own, csend, crecv,
     wl_s, a_ss, a_rs, c_ss, c_rs,
 ):
     z, xl, c, t = coords()
@@ -269,6 +271,9 @@
         dst = abuf.at[0, :, pl.ds(pl.multiple_of(half * OUT, OUT), OUT)]
         return pltpu.make_async_copy(h_ref, dst, a_rs.at[0, half])
 
+    for d in (4, 1):
+        a_send(d).start()
+
     @pl.when(here)
     def _():
         a_local().start()
@@ -277,7 +282,7 @@
     def _():
         a_send(0).start()
 
-    for d in range(1, 8):
+    for d in (6, 3, 5, 2, 7):
         a_send(d).start()
 
     for e in range(4):
@@ -288,19 +293,21 @@
         load.wait()
 
     def c_copy(ch, e):
-        return remote(acc.at[ch, e], crecv.at[ch, e - 1], c_ss.at[ch, e], c_rs.at[ch, e], z_peer(e))
-
-    own = []
+        return remote(csend.at[ch, e - 1], crecv.at[ch, e - 1], c_ss.at[ch, e], c_rs.at[ch, e], z_peer(e))
+
     for ch in range(NO):
         w = wbuf[:, :, ch * CW : (ch + 1) * CW].reshape(PLANE, CW)
         part = jnp.dot(abuf[...].reshape(4 * TOK, PLANE), w, preferred_element_type=jnp.float32)
-        acc[ch] = part.reshape(4, TOK, CW)
+        own[ch] = part[:TOK]
+        csend[ch] = part[TOK:].astype(jnp.bfloat16).reshape(3, TOK, CW)
         for e in (1, 3, 2):
             c_copy(ch, e).start()
     for ch in range(NO):
         for e in range(1, 4):
             c_copy(ch, e).wait_recv()
-        total = acc[ch, 0] + crecv[ch, 0] + crecv[ch, 1] + crecv[ch, 2]
+        total = own[ch]
+        for e in range(3):
+            total = total + crecv[ch, e].astype(jnp.float32)
         out_ref[:, ch * CW : (ch + 1) * CW] = total.astype(jnp.bfloat16)
 
     @pl.when(jnp.logical_not(here))
@@ -326,7 +333,7 @@
             jax.ShapeDtypeStruct((TOK, QKV), jnp.float32),
             jax.ShapeDtypeStruct((32, WROWS, OUT), jnp.bfloat16),
         ),
-        in_specs=[VM, VM, ANY],
+        in_specs=[ANY, ANY, ANY],
         out_specs=(VM, ANY),
         scratch_shapes=[
             pltpu.VMEM((4, TOK, PLANE), jnp.bfloat16),
@@ -353,8 +360,9 @@
         scratch_shapes=[
             pltpu.VMEM((4, TOK, PLANE), jnp.bfloat16),
             pltpu.VMEM((32, WROWS, OUT), jnp.bfloat16),
-            pltpu.VMEM((NO, 4, TOK, CW), jnp.float32),
-            pltpu.VMEM((NO, 3, TOK, CW), jnp.float32),
+            pltpu.VMEM((NO, TOK, CW), jnp.float32),
+            pltpu.VMEM((NO, 3, TOK, CW), jnp.bfloat16),
+            pltpu.VMEM((NO, 3, TOK, CW), jnp.bfloat16),
             DMA((1,)),
             DMA((8,)), DMA((4, 2)),
             DMA((NO, 4)), DMA((NO, 4)),
@@ -364,19 +372,66 @@
     )(heads, weights)
 
 
-def merge_rows(frozen_base_rows, down_stack, up_stack, adapter_slot):
-    down_rows = lax.dynamic_index_in_dim(down_stack, adapter_slot, 0, keepdims=False)
-    up_projection_rows = lax.dynamic_index_in_dim(up_stack, adapter_slot, 0, keepdims=False)
-    low_rank_delta = jnp.dot(down_rows, up_projection_rows, preferred_element_type=jnp.float32)
-    return (frozen_base_rows.astype(jnp.float32) + low_rank_scale * low_rank_delta).astype(
-        jnp.bfloat16
-    )
-
-
-def normalize(states, norm_gain):
-    widened = states.astype(jnp.float32)
+def prepare_kernel(
+    slot_ref, gain_ref, states_ref, q_ref, k_ref, v_ref, o_ref,
+    qd_ref, kd_ref, vd_ref, od_ref, qu_ref, ku_ref, vu_ref, ou_ref,
+    normed_ref, joined_ref, merged_ref,
+):
+    def merge(base, down, up):
+        delta = jnp.dot(down[0], up[0], preferred_element_type=jnp.float32)
+        return (base[...].astype(jnp.float32) + low_rank_scale * delta).astype(jnp.bfloat16)
+
+    head_cols = q_ref.shape[1]
+    kv_cols = k_ref.shape[1]
+    joined_ref[:, :head_cols] = merge(q_ref, qd_ref, qu_ref)
+    joined_ref[:, head_cols : head_cols + kv_cols] = merge(k_ref, kd_ref, ku_ref)
+    joined_ref[:, head_cols + kv_cols :] = merge(v_ref, vd_ref, vu_ref)
+    merged_ref[...] = merge(o_ref, od_ref, ou_ref)
+    widened = states_ref[...].astype(jnp.float32)
     squared_average = jnp.mean(widened * widened, axis=-1, keepdims=True)
-    return (widened * lax.rsqrt(squared_average + epsilon) * norm_gain).astype(jnp.bfloat16)
+    normed = widened * lax.rsqrt(squared_average + epsilon) * gain_ref[...].reshape(1, 1, -1)
+    normed_ref[...] = normed.reshape(normed_ref.shape).astype(jnp.bfloat16)
+
+
+def prepare(slot, gain, states, bases, downs, ups):
+    steps = 8
+    seqs, decode, width = states.shape
+    block = seqs // steps
+
+    def cols(array):
+        return pl.BlockSpec((array.shape[0], array.shape[1] // steps), lambda i, s: (0, i))
+
+    def down(array):
+        return pl.BlockSpec((1, *array.shape[1:]), lambda i, s: (s[0], 0, 0))
+
+    def up(array):
+        return pl.BlockSpec((1, array.shape[1], array.shape[2] // steps), lambda i, s: (s[0], 0, i))
+
+    return pl.pallas_call(
+        prepare_kernel,
+        out_shape=(
+            jax.ShapeDtypeStruct((seqs * decode, width), jnp.bfloat16),
+            jax.ShapeDtypeStruct((WROWS, QKV * steps), jnp.bfloat16),
+            jax.ShapeDtypeStruct((WROWS, OUT * steps), jnp.bfloat16),
+        ),
+        grid_spec=pltpu.PrefetchScalarGridSpec(
+            num_scalar_prefetch=1,
+            grid=(steps,),
+            in_specs=[
+                pl.BlockSpec((1, width), lambda i, s: (0, 0)),
+                pl.BlockSpec((block, decode, width), lambda i, s: (i, 0, 0)),
+                *[cols(b) for b in bases],
+                *[down(d) for d in downs],
+                *[up(u) for u in ups],
+            ],
+            out_specs=(
+                pl.BlockSpec((block * decode, width), lambda i, s: (i, 0)),
+                pl.BlockSpec((WROWS, QKV), lambda i, s: (0, i)),
+                pl.BlockSpec((WROWS, OUT), lambda i, s: (0, i)),
+            ),
+        ),
+        name="prepare",
+    )(slot, gain.reshape(1, -1), states, *bases, *downs, *ups)
 
 
 def rotate(vectors, positions):
@@ -446,23 +501,16 @@
     cache_keys,
     cache_values,
 ):
-    adapter_slot = adapter_layer[0]
     tp_size = lax.axis_size("tp")
-    row_count = query_base.shape[0]
-    merged_query = merge_rows(query_base, query_down, query_up, adapter_slot)
-    merged_key = merge_rows(key_base, key_down, key_up, adapter_slot)
-    merged_value = merge_rows(value_base, value_down, value_up, adapter_slot)
-    merged_output = merge_rows(output_base, output_down, output_up, adapter_slot)
-    joined = jnp.concatenate(
-        (
-            merged_query.reshape(row_count, tp_size, -1),
-            merged_key.reshape(row_count, tp_size, -1),
-            merged_value.reshape(row_count, tp_size, -1),
-        ),
-        2,
-    ).reshape(row_count, -1)
-    seq_count, step_count, model_width = states.shape
-    normed = normalize(states, norm_gain).reshape(seq_count * step_count, model_width)
+    seq_count, step_count, _ = states.shape
+    normed, joined, merged_output = prepare(
+        adapter_layer,
+        norm_gain,
+        states,
+        (query_base, key_base, value_base, output_base),
+        (query_down, key_down, value_down, output_down),
+        (query_up, key_up, value_up, output_up),
+    )
     projected, output_rows = project(normed, joined, merged_output)
     head_cols = HQ * DH // tp_size
     kv_cols = KVH * DH // tp_size

time: 201 us -> 149 us (0.74)
  the two profiles are of different devices: /device:TPU:32 before, /device:TPU:60 now
where the time goes in v2:
time: 149 us; the launch traced here: 147 us
  Pallas kernels  133 us (89%)
  local copies, waits for them, and re-layouts  6.49 us (4%)
  matrix products  4.08 us (3%)
  other arithmetic  2.47 us (2%)
    pallas_call x1, Pallas kernels, project(): pl.pallas_call(project_kernel, out_shape=(jax.ShapeDtypeStruct((TOK, QKV)...  62.7 us
    pallas_call x1, Pallas kernels, output_projection(): pl.pallas_call(output_kernel, out_shape=jax.ShapeDtypeStruct((TOK, OUT),...  61.8 us
    pallas_call x1, Pallas kernels, prepare(): pl.pallas_call(prepare_kernel, out_shape=(jax.ShapeDtypeStruct((seqs * de...  8.43 us
    unnamed x15, local copies, waits for them, and re-layouts  5.22 us

profile of v2, /device:TPU:60, one launch (start us, length us, event | category | flops | bytes accessed | tf_op | source)
XLA Modules:
  0.0 146.8 jit_solution(13728840203184360236)
XLA Ops:
  0.7 8.4 %prepare.1 = (bf16[128,8192]{1,0:T(8,128)(2,1)}, bf16[64,10240]{1,0:T(8,128)(2,1)}, bf16[64,8192]{1,0:T(8,128)(2,1)}) custom-call(s32[1]{0:T(128)S(6)} %copy.26.slot_ref, f32[1,8192]{1,0:T(1,128)} %bitcast.72, bf16[32,4,8192]{2,1,0:T(4,128)(2,1)} %states_ref.1, bf16[64,8192]{1,0:T(8,128)(2,1)} %q_ref.1, bf16[64,1024]{1,0:T(8,128)(2,1)} %k_ref.1, ...), custom_call_target="tpu_custom_call" | custom-call | tf_op jit(solution)/shard_map/prepare/pallas_call | solution.py:410
  9.1 0.0 copy-start.1
  9.1 1.6 %copy-done.1 = bf16[128,8192]{1,0:T(8,128)(2,1)S(1)} copy-done((bf16[128,8192]{1,0:T(8,128)(2,1)S(1)}, bf16[128,8192]{1,0:T(8,128)(2,1)}, u32[]{:S(2)}) %copy-start.1) | copy-done | bytes 2097176
  10.7 1.3 copy-done.2
  12.0 1.2 copy-done.3
  13.2 62.7 %project.1 = (f32[128,1280]{1,0:T(8,128)S(1)}, bf16[32,64,1024]{2,1,0:T(8,128)(2,1)}) custom-call(bf16[128,8192]{1,0:T(8,128)(2,1)S(1)} %copy-done.1, bf16[64,10240]{1,0:T(8,128)(2,1)S(1)} %copy-done.2, bf16[64,8192]{1,0:T(8,128)(2,1)S(1)} %copy-done.3), custom_call_target="tpu_custom_call" | custom-call | tf_op jit(solution)/shard_map/project/pallas_call | solution.py:330
  75.9 0.2 reshape.161
  76.1 0.0 copy-start.5
  76.1 0.1 slice.29
  76.2 0.2 reshape.162
  76.4 0.0 copy-start.4
  76.4 0.2 slice_negate_fusion
  76.7 0.1 copy-done.5
  76.8 0.1 iota_add_fusion
  76.9 0.5 multiply_cosine_fusion
  77.4 0.1 pad_maximum_fusion
  77.6 0.2 fusion.17
  77.8 0.1 fusion.21
  77.9 1.3 fusion.30
  79.3 0.1 iota_compare_fusion
  79.3 0.0 copy-done.4
  79.4 0.0 copy-start.6
  79.4 1.6 %fusion.29 = (f32[32,4,8]{2,1,0:T(4,128)S(1)}, f32[32,4,1,8,512]{4,3,1,0,2:T(8,128)S(1)}) fusion(bf16[32,4,8,128]{3,2,1,0:T(8,128)(2,1)S(1)} %fusion.17, bf16[32,512,1,128]{3,1,2,0:T(8,128)(2,1)S(1)} %copy-done.4, pred[32,512]{1,0:T(8,128)(4,1)S(1)} %iota_compare_fusion), kind=kOutput, calls=%fused_computation.46 | convolution fusion | flops 135789568 | bytes 6574080 | tf_op jit(solution)/shard_map/bskgd,blkd->bskgl/dot_general | solution.py:458
  80.9 0.3 fusion.18
  81.2 0.8 fusion.5
  82.0 0.0 copy-done.6
  82.0 0.0 copy-start
  82.0 0.9 fusion.8
  82.9 0.4 fusion.11
  83.3 0.9 copy-done
  84.2 61.8 %output_projection.1 = bf16[128,1024]{1,0:T(8,128)(2,1)S(1)} custom-call(bf16[128,1024]{1,0:T(8,128)(2,1)S(1)} %bitcast.70, bf16[32,64,1024]{2,1,0:T(8,128)(2,1)S(1)} %copy-done), custom_call_target="tpu_custom_call" | custom-call | tf_op jit(solution)/shard_map/output_projection/pallas_call | solution.py:355
  146.0 0.8 reshape.168
  (9 shorter events, 0.1 us)
Async XLA Ops:
  9.1 1.6 %copy-start.1 = (bf16[128,8192]{1,0:T(8,128)(2,1)S(1)}, bf16[128,8192]{1,0:T(8,128)(2,1)}, u32[]{:S(2)}) copy-start(bf16[128,8192]{1,0:T(8,128)(2,1)} %get-tuple-element.10.a_ref) | copy-start | bytes 6291460
  10.7 1.3 copy-start.2
  12.0 1.2 copy-start.3
  76.1 0.7 copy-start.5
  76.4 2.9 %copy-start.4 = (bf16[32,512,1,128]{3,1,2,0:T(8,128)(2,1)S(1)}, bf16[32,512,1,128]{3,1,2,0:T(8,128)(2,1)}, u32[]{:S(2)}) copy-start(bf16[32,512,1,128]{3,1,2,0:T(8,128)(2,1)} %param.34) | copy-start | bytes 12582916
  79.4 2.7 %copy-start.6 = (bf16[32,512,1,128]{3,1,2,0:T(8,128)(2,1)S(1)}, bf16[32,512,1,128]{3,1,2,0:T(8,128)(2,1)}, u32[]{:S(2)}) copy-start(bf16[32,512,1,128]{3,1,2,0:T(8,128)(2,1)} %param.35) | copy-start | bytes 12582916
  82.0 2.2 %copy-start = (bf16[32,64,1024]{2,1,0:T(8,128)(2,1)S(1)}, bf16[32,64,1024]{2,1,0:T(8,128)(2,1)}, u32[]{:S(2)}) copy-start(bf16[32,64,1024]{2,1,0:T(8,128)(2,1)} %get-tuple-element.14.wo_ref) | copy-start | bytes 12582916

commit v3 on v2

v3 whole, which is shorter than its diff:
```python
import functools

import jax
import jax.numpy as jnp
from jax import lax
from jax.experimental import pallas as pl
from jax.experimental.pallas import tpu as pltpu
from jax.sharding import PartitionSpec as P

HQ = 64
KVH = 8
DH = 128
LEN = 512
STEPS = 4
MESH = pl.DeviceIdType.MESH

rope_theta = 1000000.0
low_rank_scale = 0.5
epsilon = 1e-06

TOK = 128
WROWS = 64
PLANE = 2048
QKV = 1280
OUT = 1024
CW = 256
NC = QKV // CW
NO = OUT // CW


def coords():
    f = lax.axis_index("fsdp")
    t = lax.axis_index("tp")
    return f // 4, lax.rem(f // 2, 2), lax.rem(f, 2), t


def flip(v, bit):
    return 1 - v if bit else v


def xor_z(z, e):
    hi, lo = z // 2, lax.rem(z, 2)
    return flip(hi, e >> 1) * 2 + flip(lo, e & 1)


def xor_t(t, d):
    b2, b1, b0 = t // 4, lax.rem(t // 2, 2), lax.rem(t, 2)
    return flip(b2, (d >> 2) & 1) * 4 + flip(b1, (d >> 1) & 1) * 2 + flip(b0, d & 1)


def dev(z, xl, c, t):
    return ((z * 2 + xl) * 2 + c, t)


def remote(src, dst, ssem, rsem, device):
    return pltpu.make_async_remote_copy(
        src_ref=src, dst_ref=dst, send_sem=ssem, recv_sem=rsem, device_id=device, device_id_type=MESH
    )


def layer_kernel(
    a_ref, w_ref, o_ref, cos_ref, sin_ref, len_ref, k_ref, v_ref, out_ref,
    abuf, wbuf, acc, crecv, ostage, wo_ref, kbuf, vbuf, qbuf, knew, vnew, mixed, heads, hbuf, dsend, drecv,
    a_ss, a_rs, w1_ss, w1_rs, w2_ss, w2_rs, w3_ss, w3_rs, c_ss, c_rs,
    o1_ss, o1_rs, r1_ss, r1_rs, r2_ss, r2_rs, r3_ss, r3_rs,
    kv_s, h_ss, h_rs, d_ss, d_rs,
):
    z, xl, c, t = coords()
    xh = t // 4
    y = lax.rem(t, 4)
    xpart = dev(z, 1 - xl, c, t)
    xcross = dev(z, 1 - xl, c, y + 4 * (1 - xh))
    ring = (xpart, xcross)
    cpart = dev(z, xl, 1 - c, t)

    def plane_peer(d):
        return dev(z, flip(xl, d >> 2), c, xor_t(t, d))

    def z_peer(e):
        return dev(xor_z(z, e), xl, c, t)

    zd = t // 2
    half = lax.rem(t, 2)

    def parity(*bits):
        return lax.rem(sum(bits), 2)

    x_to = parity(xh, z, y // 2)
    here = (z == zd) & (xh == x_to)

    def h_target(d):
        return dev(zd, xl, c, x_to * 4 + xor_t(y, d))

    odd = parity(xh, z // 2, z)

    def h_source(i, h):
        return dev(2 * i + odd, xl, c, 2 * z + h)

    def d_target(i, j):
        return dev(2 * i + odd, xl, c, j * 4 + y)

    def d_source(p):
        return dev(p, xl, c, parity(z, p // 2, p) * 4 + y)

    cache = [
        pltpu.make_async_copy(k_ref, kbuf, kv_s.at[0]),
        pltpu.make_async_copy(v_ref, vbuf, kv_s.at[1]),
    ]

    barrier = pltpu.get_barrier_semaphore()
    peers = [plane_peer(d) for d in range(1, 8)] + [z_peer(e) for e in range(1, 4)] + [xpart, cpart, xcross]
    peers += [h_target(d) for d in range(4)] + [d_source(p) for p in range(4)]
    peers += [h_source(i, h) for i in range(2) for h in range(2)]
    peers += [d_target(i, j) for i in range(2) for j in range(2)]
    for p in peers:
        pl.semaphore_signal(barrier, inc=1, device_id=p, device_id_type=MESH)
    pl.semaphore_wait(barrier, len(peers))

    def a_copy(e):
        cols = pl.ds(pl.multiple_of(xor_z(z, e) * PLANE, PLANE), PLANE)
        if e == 0:
            return pltpu.make_async_copy(a_ref.at[:, cols], abuf.at[0], a_rs.at[0])
        return remote(a_ref.at[:, cols], abuf.at[e], a_ss.at[e], a_rs.at[e], z_peer(e))

    my_slot = (xl * 2 + c) * 8 + t

    def w1_copy(ch, d):
        td = xor_t(t, d)
        cols = pl.ds(pl.multiple_of(td * QKV + ch * CW, CW), CW)
        src = w_ref.at[:, cols]
        dst = wbuf.at[ch, my_slot]
        if d == 0:
            return pltpu.make_async_copy(src, dst, w1_rs.at[ch, 0])
        return remote(src, dst, w1_ss.at[ch, d], w1_rs.at[ch, d], plane_peer(d))

    def o_slot(source, d):
        lo = xl if source in (0, 3) else 1 - xl
        hi = xh if source in (0, 1) else 1 - xh
        return lo, hi, xor_t(y, d)

    def o_rows(source, d, core):
        lo, hi, row = o_slot(source, d)
        return wo_ref.at[(lo * 2 + core) * 8 + hi * 4 + row]

    def o_mine(d):
        return o_ref.at[:, pl.ds(pl.multiple_of(xor_t(y, d) * 2 * OUT, 2 * OUT), 2 * OUT)]

    def o1_copy(d):
        if d == 0:
            return pltpu.make_async_copy(o_mine(0), ostage, o1_rs.at[0])
        return remote(o_mine(d), wo_ref.at[my_slot], o1_ss.at[d], o1_rs.at[d], dev(z, xl, c, xh * 4 + xor_t(y, d)))

    def o1_wait(d):
        ref = o_rows(0, d, c)
        remote(ref, ref, o1_ss.at[d], o1_rs.at[d], xpart).wait_recv()

    def o_keep():
        return pltpu.make_async_copy(ostage, wo_ref.at[my_slot], o1_ss.at[0])

    def r1_copy(n, d):
        src = ostage if d == 0 else o_rows(0, d, c)
        return remote(src, o_rows(0, d, c), r1_ss.at[n, d], r1_rs.at[n, d], ring[n])

    def r1_wait(n, d):
        ref = o_rows(1 + n, d, c)
        remote(ref, ref, r1_ss.at[n, d], r1_rs.at[n, d], ring[n]).wait_recv()

    def r2_copy(d):
        n = 0 if d == 2 else 1
        ref = o_rows(2 - n, d, c)
        return remote(ref, ref, r2_ss.at[d], r2_rs.at[d], ring[n])

    def r2_wait(d):
        ref = o_rows(3, d, c)
        remote(ref, ref, r2_ss.at[d], r2_rs.at[d], xpart).wait_recv()

    def r3_copy(source, d):
        ref = o_rows(source, d, c)
        src = ostage if (source, d) == (0, 0) else ref
        return remote(src, ref, r3_ss.at[source, d], r3_rs.at[source, d], cpart)

    def r3_wait(source, d):
        ref = o_rows(source, d, 1 - c)
        remote(ref, ref, r3_ss.at[source, d], r3_rs.at[source, d], cpart).wait_recv()

    def group_base(g, core):
        lo = xl if g in (0, 3) else 1 - xl
        hi = xh if g in (0, 2) else 1 - xh
        return (lo * 2 + core) * 8 + hi * 4

    def w2_copy(k, g):
        ref = wbuf.at[k, pl.ds(group_base(g, c), 4)]
        return remote(ref, ref, w2_ss.at[k, g], w2_rs.at[k, g], xpart)

    def w2_wait(k, g):
        ref = wbuf.at[k, pl.ds(group_base(g + 2, c), 4)]
        remote(ref, ref, w2_ss.at[k, g], w2_rs.at[k, g], xpart).wait_recv()

    def w3_copy(k, g):
        ref = wbuf.at[k, pl.ds(group_base(g, c), 4)]
        return remote(ref, ref, w3_ss.at[k, g], w3_rs.at[k, g], cpart)

    def w3_wait(k, g):
        ref = wbuf.at[k, pl.ds(group_base(g, 1 - c), 4)]
        remote(ref, ref, w3_ss.at[k, g], w3_rs.at[k, g], cpart).wait_recv()

    def c_copy(ch, e):
        return remote(acc.at[ch, e], crecv.at[ch, e - 1], c_ss.at[ch, e], c_rs.at[ch, e], z_peer(e))

    def start_w1(ch, carry):
        for d in range(8):
            w1_copy(ch, d).start()
        return carry

    start_w1(0, 0)
    for e in (1, 3, 2, 0):
        a_copy(e).start()
    o1_copy(0).start()
    for copy in cache:
        copy.start()
    lax.fori_loop(1, NC, start_w1, 0)
    for d in (1, 3, 2):
        o1_copy(d).start()

    def relay(k):
        for g in range(2):
            for d in range(g * 4, g * 4 + 4):
                source_slot = (flip(xl, d >> 2) * 2 + c) * 8 + xor_t(t, d)
                if d == 0:
                    w1_copy(k, 0).wait()
                else:
                    ref = wbuf.at[k, source_slot]
                    remote(ref, ref, w1_ss.at[k, d], w1_rs.at[k, d], plane_peer(d)).wait_recv()
            w2_copy(k, g).start()
            w3_copy(k, g).start()

    def share(k):
        for g in range(2):
            w2_wait(k, g)
            w3_copy(k, g + 2).start()

    def multiply(ch):
        for g in range(4):
            w3_wait(ch, g)
        rows = abuf[...].reshape(4 * TOK, PLANE)
        part = jnp.dot(rows, wbuf[ch].reshape(PLANE, CW), preferred_element_type=jnp.float32)
        acc[ch] = part.reshape(4, TOK, CW)
        for e in (1, 3, 2):
            c_copy(ch, e).start()

    relay(0)
    o1_copy(0).wait()
    r1_copy(1, 0).start()
    r3_copy(0, 0).start()
    o_keep().start()
    for ch in range(3):
        relay(ch + 1)
        share(ch)
    r1_copy(0, 0).start()
    relay(4)
    share(3)
    a_copy(0).wait()
    for e in (1, 3, 2):
        a_copy(e).wait_recv()
    multiply(0)
    multiply(1)

    def spread(d):
        o1_wait(d)
        r1_copy(1, d).start()
        r1_copy(0, d).start()
        r3_copy(0, d).start()

    spread(1)
    multiply(2)
    spread(3)
    multiply(3)
    spread(2)
    share(4)
    multiply(4)

    def forward(d):
        n = 0 if d == 2 else 1
        r1_wait(1 - n, d)
        r2_copy(d).start()
        r3_copy(2 - n, d).start()

    def keep(d):
        n = 1 if d == 2 else 0
        r1_wait(1 - n, d)
        r3_copy(2 - n, d).start()

    forward(0)
    keep(0)
    keep(1)
    keep(3)
    forward(2)
    forward(1)
    forward(3)
    keep(2)
    def rope(values):
        return values * cos_ref[...] + pltpu.roll(values, DH // 2, axis=1) * sin_ref[...]

    for ch in range(NC):
        for e in range(1, 4):
            c_copy(ch, e).wait_recv()
        part = acc[ch, 0] + crecv[ch, 0] + crecv[ch, 1] + crecv[ch, 2]
        first, second = part[:, :DH], part[:, DH:]
        if ch < NC - 1:
            qbuf[2 * ch] = rope(first).astype(jnp.bfloat16).astype(jnp.float32)
            qbuf[2 * ch + 1] = rope(second).astype(jnp.bfloat16).astype(jnp.float32)
        else:
            knew[...] = rope(first).astype(jnp.bfloat16)
            vnew[...] = second.astype(jnp.bfloat16)
    for copy in cache:
        copy.wait()

    score_scale = DH ** (-0.5)
    contract_last = (((1,), (1,)), ((), ()))

    def attend_pair(p):
        tokens = pl.ds(pl.multiple_of(p * 8, 8), 8)
        queries = qbuf[:, tokens, :].reshape(64, DH).astype(jnp.bfloat16)
        keys = kbuf[pl.ds(2 * p, 2)].reshape(2 * LEN, DH)
        values = vbuf[pl.ds(2 * p, 2)].reshape(2 * LEN, DH)
        token = lax.rem(lax.broadcasted_iota(jnp.int32, (64, 1), 0), 8)
        second = token >= STEPS
        low = jnp.where(second, LEN, 0)
        high = low + jnp.where(second, len_ref[2 * p + 1], len_ref[2 * p])
        slot = lax.broadcasted_iota(jnp.int32, (64, 2 * LEN), 1)
        old = lax.dot_general(queries, keys, contract_last, preferred_element_type=jnp.float32) * score_scale
        old = jnp.where((slot >= low) & (slot < high), old, -1e30)
        column = lax.broadcasted_iota(jnp.int32, (64, TOK), 1)
        last = p * 8 + token
        begin = p * 8 + jnp.where(second, STEPS, 0)
        new = lax.dot_general(queries, knew[...], contract_last, preferred_element_type=jnp.float32) * score_scale
        new = jnp.where((column >= begin) & (column <= last), new, -1e30)
        highest = jnp.maximum(jnp.max(old, -1, keepdims=True), jnp.max(new, -1, keepdims=True))
        old_exp = jnp.exp(old - highest)
        new_exp = jnp.exp(new - highest)
        inverse = 1.0 / (jnp.sum(old_exp, -1, keepdims=True) + jnp.sum(new_exp, -1, keepdims=True))
        old_weights = (old_exp * inverse).astype(jnp.bfloat16)
        new_weights = (new_exp * inverse).astype(jnp.bfloat16)
        mixture = jnp.dot(old_weights, values, preferred_element_type=jnp.float32)
        mixture = mixture + jnp.dot(new_weights, vnew[...], preferred_element_type=jnp.float32)
        for g in range(8):
            mixed[tokens, g * DH : (g + 1) * DH] = mixture[g * 8 : (g + 1) * 8]

    QT = TOK // 4

    def h_rows(qt):
        return heads.at[pl.ds(pl.multiple_of(qt * QT, QT), QT)]

    def h_slot(qt):
        return hbuf.at[z // 2, pl.ds(pl.multiple_of(qt * QT, QT), QT), pl.ds(pl.multiple_of(half * OUT, OUT), OUT)]

    def h_send(qt, d):
        return remote(h_rows(qt), h_slot(qt), h_ss.at[qt, d], h_rs.at[z // 2, half, qt], h_target(d))

    def h_local(qt):
        return pltpu.make_async_copy(h_rows(qt), h_slot(qt), h_rs.at[z // 2, half, qt])

    def quarter(qt, carry):
        for n in range(4):
            attend_pair(qt * 4 + n)
        rows = pl.ds(pl.multiple_of(qt * QT, QT), QT)
        heads[rows] = mixed[rows].astype(jnp.bfloat16)
        for d in (2, 1, 3):
            h_send(qt, d).start()

        @pl.when(here)
        def _():
            h_local(qt).start()

        @pl.when(jnp.logical_not(here))
        def _():
            h_send(qt, 0).start()

        return carry

    lax.fori_loop(0, 4, quarter, 0)

    for d in (0, 1, 3, 2):
        r2_wait(d)
        r3_copy(3, d).start()
    for source in range(4):
        for d in range(4):
            r3_wait(source, d)
    o_keep().wait()

    for i in range(2):
        for h in range(2):
            for qt in range(4):
                ref = hbuf.at[i, pl.ds(qt * QT, QT), pl.ds(h * OUT, OUT)]
                pltpu.make_async_copy(ref, ref, h_rs.at[i, h, qt]).wait()

    def mine(i, j):
        return (2 * i + odd == z) & (xh == j)

    def d_copy(n, j, i):
        return remote(
            dsend.at[j, n, i], drecv.at[n, z], d_ss.at[j, n, i], d_rs.at[n, z], d_target(i, j)
        )

    def d_local(n, j, i):
        return pltpu.make_async_copy(dsend.at[j, n, i], drecv.at[n, z], d_rs.at[n, z])

    for n in range(NO):
        for j in range(2):
            lo = j * OUT + n * CW
            w = wo_ref[:, :, lo : lo + CW].reshape(PLANE, CW)
            part = jnp.dot(hbuf[...].reshape(2 * TOK, PLANE), w, preferred_element_type=jnp.float32)
            dsend[j, n] = part.astype(jnp.bfloat16).reshape(2, TOK, CW)
            for i in range(2):

                @pl.when(mine(i, j))
                def _():
                    d_local(n, j, i).start()

                @pl.when(jnp.logical_not(mine(i, j)))
                def _():
                    d_copy(n, j, i).start()

    for n in range(NO):
        total = None
        for p in range(4):
            ref = drecv.at[n, p]
            pltpu.make_async_copy(ref, ref, d_rs.at[n, p]).wait()
            part = drecv[n, p].astype(jnp.float32)
            total = part if total is None else total + part
        out_ref[:, :, n * CW : (n + 1) * CW] = total.reshape(TOK // STEPS, STEPS, CW).astype(jnp.bfloat16)

    def drain_heads(qt, carry):
        for d in range(1, 4):
            h_send(qt, d).wait_send()

        @pl.when(jnp.logical_not(here))
        def _():
            h_send(qt, 0).wait_send()

        return carry

    lax.fori_loop(0, 4, drain_heads, 0)
    for n in range(NO):
        for j in range(2):
            for i in range(2):

                @pl.when(jnp.logical_not(mine(i, j)))
                def _():
                    d_copy(n, j, i).wait_send()

    for e in range(1, 4):
        a_copy(e).wait_send()

    def drain(ch, carry):
        for d in range(1, 8):
            w1_copy(ch, d).wait_send()
        for g in range(2):
            w2_copy(ch, g).wait_send()
        for g in range(4):
            w3_copy(ch, g).wait_send()
        for e in range(1, 4):
            c_copy(ch, e).wait_send()
        return carry

    lax.fori_loop(0, NC, drain, 0)
    for d in range(1, 4):
        o1_copy(d).wait_send()
    for d in range(4):
        r1_copy(0, d).wait_send()
        r1_copy(1, d).wait_send()
        r2_copy(d).wait_send()
        for source in range(4):
            r3_copy(source, d).wait_send()


VM = pl.BlockSpec(memory_space=pltpu.VMEM)
ANY = pl.BlockSpec(memory_space=pl.ANY)
DMA = pltpu.SemaphoreType.DMA


def run_layer(normed, joined, merged_output, cosine, sine, lengths, keys, values):
    return pl.pallas_call(
        layer_kernel,
        out_shape=jax.ShapeDtypeStruct((TOK // STEPS, STEPS, OUT), jnp.bfloat16),
        in_specs=[ANY, ANY, ANY, VM, VM, pl.BlockSpec(memory_space=pltpu.SMEM), ANY, ANY],
        out_specs=VM,
        scratch_shapes=[
            pltpu.VMEM((4, TOK, PLANE), jnp.bfloat16),
            pltpu.VMEM((NC, 32, WROWS, CW), jnp.bfloat16),
            pltpu.VMEM((NC, 4, TOK, CW), jnp.float32),
            pltpu.VMEM((NC, 3, TOK, CW), jnp.float32),
            pltpu.VMEM((WROWS, 2 * OUT), jnp.bfloat16),
            pltpu.VMEM((32, WROWS, 2 * OUT), jnp.bfloat16),
            pltpu.VMEM(keys.shape, jnp.bfloat16),
            pltpu.VMEM(values.shape, jnp.bfloat16),
            pltpu.VMEM((8, TOK, DH), jnp.float32),
            pltpu.VMEM((TOK, DH), jnp.bfloat16),
            pltpu.VMEM((TOK, DH), jnp.bfloat16),
            pltpu.VMEM((TOK, OUT), jnp.float32),
            pltpu.VMEM((TOK, OUT), jnp.bfloat16),
            pltpu.VMEM((2, TOK, PLANE), jnp.bfloat16),
            pltpu.VMEM((2, NO, 2, TOK, CW), jnp.bfloat16),
            pltpu.VMEM((NO, 4, TOK, CW), jnp.bfloat16),
            DMA((4,)), DMA((4,)),
            DMA((NC, 8)), DMA((NC, 8)),
            DMA((NC, 2)), DMA((NC, 2)),
            DMA((NC, 4)), DMA((NC, 4)),
            DMA((NC, 4)), DMA((NC, 4)),
            DMA((4,)), DMA((4,)),
            DMA((2, 4)), DMA((2, 4)),
            DMA((4,)), DMA((4,)),
            DMA((4, 4)), DMA((4, 4)),
            DMA((2,)),
            DMA((4, 4)), DMA((2, 2, 4)),
            DMA((2, NO, 2)), DMA((NO, 4)),
        ],
        compiler_params=pltpu.CompilerParams(collective_id=0, has_side_effects=True, vmem_limit_bytes=62 << 20),
        name="layer",
    )(normed, joined, merged_output, cosine, sine, lengths, keys, values)


def prepare_kernel(
    slot_ref, gain_ref, states_ref, q_ref, k_ref, v_ref, o_ref,
    qd_ref, kd_ref, vd_ref, od_ref, qu_ref, ku_ref, vu_ref, ou_ref,
    normed_ref, joined_ref, merged_ref,
):
    def merge(base, down, up):
        delta = jnp.dot(down[0], up[0], preferred_element_type=jnp.float32)
        return (base[...].astype(jnp.float32) + low_rank_scale * delta).astype(jnp.bfloat16)

    head_cols = q_ref.shape[1]
    kv_cols = k_ref.shape[1]
    joined_ref[:, :head_cols] = merge(q_ref, qd_ref, qu_ref)
    joined_ref[:, head_cols : head_cols + kv_cols] = merge(k_ref, kd_ref, ku_ref)
    joined_ref[:, head_cols + kv_cols :] = merge(v_ref, vd_ref, vu_ref)
    merged_ref[...] = merge(o_ref, od_ref, ou_ref)
    widened = states_ref[...].astype(jnp.float32)
    squared_average = jnp.mean(widened * widened, axis=-1, keepdims=True)
    normed = widened * lax.rsqrt(squared_average + epsilon) * gain_ref[...].reshape(1, 1, -1)
    normed_ref[...] = normed.reshape(normed_ref.shape).astype(jnp.bfloat16)


def prepare(slot, gain, states, bases, downs, ups):
    steps = 8
    seqs, decode, width = states.shape
    block = seqs // steps

    def cols(array):
        return pl.BlockSpec((array.shape[0], array.shape[1] // steps), lambda i, s: (0, i))

    def down(array):
        return pl.BlockSpec((1, *array.shape[1:]), lambda i, s: (s[0], 0, 0))

    def up(array):
        return pl.BlockSpec((1, array.shape[1], array.shape[2] // steps), lambda i, s: (s[0], 0, i))

    return pl.pallas_call(
        prepare_kernel,
        out_shape=(
            jax.ShapeDtypeStruct((seqs * decode, width), jnp.bfloat16),
            jax.ShapeDtypeStruct((WROWS, QKV * steps), jnp.bfloat16),
            jax.ShapeDtypeStruct((WROWS, OUT * steps), jnp.bfloat16),
        ),
        grid_spec=pltpu.PrefetchScalarGridSpec(
            num_scalar_prefetch=1,
            grid=(steps,),
            in_specs=[
                pl.BlockSpec((1, width), lambda i, s: (0, 0)),
                pl.BlockSpec((block, decode, width), lambda i, s: (i, 0, 0)),
                *[cols(b) for b in bases],
                *[down(d) for d in downs],
                *[up(u) for u in ups],
            ],
            out_specs=(
                pl.BlockSpec((block * decode, width), lambda i, s: (i, 0)),
                pl.BlockSpec((WROWS, QKV), lambda i, s: (0, i)),
                pl.BlockSpec((WROWS, OUT), lambda i, s: (0, lax.rem(i, 4) * 2 + i // 4)),
            ),
        ),
        name="prepare",
    )(slot, gain.reshape(1, -1), states, *bases, *downs, *ups)


def rope_tables(positions):
    half_dim = DH // 2
    frequency = rope_theta ** (-2.0 * jnp.arange(half_dim, dtype=jnp.float32) / DH)
    rotation_phases = positions[:, None] * frequency[None, :]
    cosine, sine = jnp.cos(rotation_phases), jnp.sin(rotation_phases)
    return jnp.concatenate((cosine, cosine), -1), jnp.concatenate((-sine, sine), -1)


def local(
    states,
    norm_gain,
    query_base,
    key_base,
    value_base,
    output_base,
    query_down,
    query_up,
    key_down,
    key_up,
    value_down,
    value_up,
    output_down,
    output_up,
    adapter_layer,
    kv_lengths,
    cache_keys,
    cache_values,
):
    seq_count, step_count, _ = states.shape
    normed, joined, merged_output = prepare(
        adapter_layer,
        norm_gain,
        states,
        (query_base, key_base, value_base, output_base),
        (query_down, key_down, value_down, output_down),
        (query_up, key_up, value_up, output_up),
    )
    positions = (
        kv_lengths.astype(jnp.float32)[:, None] + jnp.arange(step_count, dtype=jnp.float32)[None, :]
    )
    cosine, sine = rope_tables(positions.reshape(-1))
    keys = cache_keys.reshape(seq_count, -1, DH)
    values = cache_values.reshape(seq_count, -1, DH)
    return run_layer(normed, joined, merged_output, cosine, sine, kv_lengths, keys, values)


def solution(mesh):
    in_specs = (
        P("fsdp", None, None),
        P(),
        P(("fsdp", "tp"), None),
        P(("fsdp", "tp"), None),
        P(("fsdp", "tp"), None),
        P(("fsdp", "tp"), None),
        P(None, ("fsdp", "tp"), None),
        P(),
        P(None, ("fsdp", "tp"), None),
        P(),
        P(None, ("fsdp", "tp"), None),
        P(),
        P(None, ("fsdp", "tp"), None),
        P(),
        P(),
        P("fsdp"),
        P("fsdp", None, "tp", None),
        P("fsdp", None, "tp", None),
    )
    out_specs = P("fsdp", None, "tp")
    return jax.shard_map(local, mesh=mesh, in_specs=in_specs, out_specs=out_specs, check_vma=False)
```

time: 149 us -> 138 us (0.926)
  the two profiles are of different devices: /device:TPU:60 before, /device:TPU:92 now
where the time goes in v3:
time: 138 us; the launch traced here: 137 us
  Pallas kernels  133 us (96%)
  local copies, waits for them, and re-layouts  1.85 us (1%)
  other arithmetic  1.8 us (1%)
    pallas_call x1, Pallas kernels, run_layer(): pl.pallas_call(layer_kernel, out_shape=jax.ShapeDtypeStruct((TOK // STEPS...  124 us
    pallas_call x1, Pallas kernels, prepare(): pl.pallas_call(prepare_kernel, out_shape=(jax.ShapeDtypeStruct((seqs * de...  8.38 us

profile of v3, /device:TPU:92, one launch (start us, length us, event | category | flops | bytes accessed | tf_op | source)
XLA Modules:
  0.0 137.2 jit_solution(8074847598636454857)
XLA Ops:
  0.7 0.7 convert_element_type.3
  1.3 0.1 iota_add_fusion
  1.4 0.1 add.23
  1.5 0.3 fusion
  1.8 0.7 pad_maximum_fusion
  2.6 8.4 %prepare.1 = (bf16[128,8192]{1,0:T(8,128)(2,1)}, bf16[64,10240]{1,0:T(8,128)(2,1)}, bf16[64,8192]{1,0:T(8,128)(2,1)}) custom-call(s32[1]{0:T(128)S(6)} %copy.20.slot_ref, f32[1,8192]{1,0:T(1,128)} %bitcast.5, bf16[32,4,8192]{2,1,0:T(4,128)(2,1)} %states_ref.1, bf16[64,8192]{1,0:T(8,128)(2,1)} %q_ref.1, bf16[64,1024]{1,0:T(8,128)(2,1)} %k_ref.1, ...), custom_call_target="tpu_custom_call" | custom-call | tf_op jit(solution)/shard_map/prepare/pallas_call | solution.py:558
  11.0 124.5 %layer.1 = bf16[32,4,1024]{2,1,0:T(4,128)(2,1)} custom-call(bf16[128,8192]{1,0:T(8,128)(2,1)} %get-tuple-element.8.a_ref, bf16[64,10240]{1,0:T(8,128)(2,1)} %get-tuple-element.9.w_ref, bf16[64,8192]{1,0:T(8,128)(2,1)} %get-tuple-element.10.o_ref, f32[128,128]{1,0:T(8,128)} %get-tuple-element.14.cos_ref, f32[128,128]{1,0:T(8,128)} %get-tuple-element.15.sin_ref, ...), custom_call_target="tpu_custom_call" | custom-call | tf_op jit(solution)/shard_map/layer/pallas_call | solution.py:483
  135.4 1.7 %copy.21 = bf16[32,4,1024]{2,1,0:T(4,128)(2,1)} copy(bf16[32,4,1024]{2,1,0:T(4,128)(2,1)} %layer.1) | data formatting | bytes 524288
  (1 shorter events, 0.0 us)

commit v4 on v3

--- a/solution.py
+++ b/solution.py
@@ -69,8 +69,10 @@
     xh = t // 4
     y = lax.rem(t, 4)
     xpart = dev(z, 1 - xl, c, t)
-    xcross = dev(z, 1 - xl, c, y + 4 * (1 - xh))
-    ring = (xpart, xcross)
+    ring = (dev(z, xl, c, xor_t(t, 1)), dev(z, xl, c, xor_t(t, 3)))
+
+    def x_peer(d):
+        return flip(xl, d & 1), flip(xh, d >> 1)
     cpart = dev(z, xl, 1 - c, t)
 
     def plane_peer(d):
@@ -82,25 +84,23 @@
     zd = t // 2
     half = lax.rem(t, 2)
 
-    def parity(*bits):
-        return lax.rem(sum(bits), 2)
-
-    x_to = parity(xh, z, y // 2)
-    here = (z == zd) & (xh == x_to)
+    y_to = lax.rem(z + 2 * (y // 2) + xh, 4)
+    here = (z == zd) & (y == y_to)
 
     def h_target(d):
-        return dev(zd, xl, c, x_to * 4 + xor_t(y, d))
-
-    odd = parity(xh, z // 2, z)
+        lo, hi = x_peer(d)
+        return dev(zd, lo, c, hi * 4 + y_to)
+
+    z_rows = lax.rem(y + 8 - 2 * lax.rem(z, 2) - z // 2, 4)
 
     def h_source(i, h):
-        return dev(2 * i + odd, xl, c, 2 * z + h)
+        return dev(z_rows, i, c, 2 * z + h)
 
     def d_target(i, j):
-        return dev(2 * i + odd, xl, c, j * 4 + y)
+        return dev(z_rows, i, c, xh * 4 + 2 * xl + j)
 
     def d_source(p):
-        return dev(p, xl, c, parity(z, p // 2, p) * 4 + y)
+        return dev(p, y // 2, c, xh * 4 + lax.rem(z + 2 * (p % 2) + p // 2, 4))
 
     cache = [
         pltpu.make_async_copy(k_ref, kbuf, kv_s.at[0]),
@@ -108,7 +108,7 @@
     ]
 
     barrier = pltpu.get_barrier_semaphore()
-    peers = [plane_peer(d) for d in range(1, 8)] + [z_peer(e) for e in range(1, 4)] + [xpart, cpart, xcross]
+    peers = [plane_peer(d) for d in range(1, 8)] + [z_peer(e) for e in range(1, 4)] + [xpart, cpart, dev(z, xl, c, xor_t(t, 4))]
     peers += [h_target(d) for d in range(4)] + [d_source(p) for p in range(4)]
     peers += [h_source(i, h) for i in range(2) for h in range(2)]
     peers += [d_target(i, j) for i in range(2) for j in range(2)]
@@ -133,22 +133,19 @@
             return pltpu.make_async_copy(src, dst, w1_rs.at[ch, 0])
         return remote(src, dst, w1_ss.at[ch, d], w1_rs.at[ch, d], plane_peer(d))
 
-    def o_slot(source, d):
-        lo = xl if source in (0, 3) else 1 - xl
-        hi = xh if source in (0, 1) else 1 - xh
-        return lo, hi, xor_t(y, d)
-
     def o_rows(source, d, core):
-        lo, hi, row = o_slot(source, d)
-        return wo_ref.at[(lo * 2 + core) * 8 + hi * 4 + row]
+        lo, hi = x_peer(d)
+        return wo_ref.at[(lo * 2 + core) * 8 + hi * 4 + xor_t(y, (0, 1, 3, 2)[source])]
 
     def o_mine(d):
-        return o_ref.at[:, pl.ds(pl.multiple_of(xor_t(y, d) * 2 * OUT, 2 * OUT), 2 * OUT)]
+        lo, hi = x_peer(d)
+        return o_ref.at[:, pl.ds(pl.multiple_of((hi * 2 + lo) * 2 * OUT, 2 * OUT), 2 * OUT)]
 
     def o1_copy(d):
         if d == 0:
             return pltpu.make_async_copy(o_mine(0), ostage, o1_rs.at[0])
-        return remote(o_mine(d), wo_ref.at[my_slot], o1_ss.at[d], o1_rs.at[d], dev(z, xl, c, xh * 4 + xor_t(y, d)))
+        lo, hi = x_peer(d)
+        return remote(o_mine(d), wo_ref.at[my_slot], o1_ss.at[d], o1_rs.at[d], dev(z, lo, c, hi * 4 + y))
 
     def o1_wait(d):
         ref = o_rows(0, d, c)
@@ -166,7 +163,7 @@
         remote(ref, ref, r1_ss.at[n, d], r1_rs.at[n, d], ring[n]).wait_recv()
 
     def r2_copy(d):
-        n = 0 if d == 2 else 1
+        n = d >> 1
         ref = o_rows(2 - n, d, c)
         return remote(ref, ref, r2_ss.at[d], r2_rs.at[d], ring[n])
 
@@ -248,56 +245,58 @@
         for e in (1, 3, 2):
             c_copy(ch, e).start()
 
+    def spread(d):
+        o1_wait(d)
+        r1_copy(0, d).start()
+        r1_copy(1, d).start()
+        r3_copy(0, d).start()
+
+    def forward(d):
+        n = d >> 1
+        r1_wait(1 - n, d)
+        r2_copy(d).start()
+        r3_copy(2 - n, d).start()
+
+    def keep(d):
+        n = 1 - (d >> 1)
+        r1_wait(1 - n, d)
+        r3_copy(2 - n, d).start()
+
     relay(0)
     o1_copy(0).wait()
+    r1_copy(0, 0).start()
     r1_copy(1, 0).start()
     r3_copy(0, 0).start()
     o_keep().start()
-    for ch in range(3):
-        relay(ch + 1)
-        share(ch)
-    r1_copy(0, 0).start()
+    relay(1)
+    share(0)
+    spread(1)
+    relay(2)
+    share(1)
+    spread(3)
+    relay(3)
+    share(2)
+    spread(2)
     relay(4)
-    share(3)
     a_copy(0).wait()
     for e in (1, 3, 2):
         a_copy(e).wait_recv()
     multiply(0)
+    share(3)
     multiply(1)
-
-    def spread(d):
-        o1_wait(d)
-        r1_copy(1, d).start()
-        r1_copy(0, d).start()
-        r3_copy(0, d).start()
-
-    spread(1)
+    forward(0)
+    keep(0)
     multiply(2)
-    spread(3)
+    forward(1)
+    keep(1)
     multiply(3)
-    spread(2)
     share(4)
     multiply(4)
-
-    def forward(d):
-        n = 0 if d == 2 else 1
-        r1_wait(1 - n, d)
-        r2_copy(d).start()
-        r3_copy(2 - n, d).start()
-
-    def keep(d):
-        n = 1 if d == 2 else 0
-        r1_wait(1 - n, d)
-        r3_copy(2 - n, d).start()
-
-    forward(0)
-    keep(0)
-    keep(1)
+    forward(3)
     keep(3)
     forward(2)
-    forward(1)
-    forward(3)
     keep(2)
+
     def rope(values):
         return values * cos_ref[...] + pltpu.roll(values, DH // 2, axis=1) * sin_ref[...]
 
@@ -352,13 +351,13 @@
         return heads.at[pl.ds(pl.multiple_of(qt * QT, QT), QT)]
 
     def h_slot(qt):
-        return hbuf.at[z // 2, pl.ds(pl.multiple_of(qt * QT, QT), QT), pl.ds(pl.multiple_of(half * OUT, OUT), OUT)]
+        return hbuf.at[xl, pl.ds(pl.multiple_of(qt * QT, QT), QT), pl.ds(pl.multiple_of(half * OUT, OUT), OUT)]
 
     def h_send(qt, d):
-        return remote(h_rows(qt), h_slot(qt), h_ss.at[qt, d], h_rs.at[z // 2, half, qt], h_target(d))
+        return remote(h_rows(qt), h_slot(qt), h_ss.at[qt, d], h_rs.at[xl, half, qt], h_target(d))
 
     def h_local(qt):
-        return pltpu.make_async_copy(h_rows(qt), h_slot(qt), h_rs.at[z // 2, half, qt])
+        return pltpu.make_async_copy(h_rows(qt), h_slot(qt), h_rs.at[xl, half, qt])
 
     def quarter(qt, carry):
         for n in range(4):
@@ -395,7 +394,7 @@
                 pltpu.make_async_copy(ref, ref, h_rs.at[i, h, qt]).wait()
 
     def mine(i, j):
-        return (2 * i + odd == z) & (xh == j)
+        return (z_rows == z) & (xl == i) & (y == 2 * xl + j)
 
     def d_copy(n, j, i):
         return remote(
@@ -529,11 +528,12 @@
         delta = jnp.dot(down[0], up[0], preferred_element_type=jnp.float32)
         return (base[...].astype(jnp.float32) + low_rank_scale * delta).astype(jnp.bfloat16)
 
-    head_cols = q_ref.shape[1]
-    kv_cols = k_ref.shape[1]
-    joined_ref[:, :head_cols] = merge(q_ref, qd_ref, qu_ref)
-    joined_ref[:, head_cols : head_cols + kv_cols] = merge(k_ref, kd_ref, ku_ref)
-    joined_ref[:, head_cols + kv_cols :] = merge(v_ref, vd_ref, vu_ref)
+    q, k, v = merge(q_ref, qd_ref, qu_ref), merge(k_ref, kd_ref, ku_ref), merge(v_ref, vd_ref, vu_ref)
+    for n in range(joined_ref.shape[1] // QKV):
+        base = n * QKV
+        joined_ref[:, base : base + OUT] = q[:, n * OUT : (n + 1) * OUT]
+        joined_ref[:, base + OUT : base + OUT + DH] = k[:, n * DH : (n + 1) * DH]
+        joined_ref[:, base + OUT + DH : base + QKV] = v[:, n * DH : (n + 1) * DH]
     merged_ref[...] = merge(o_ref, od_ref, ou_ref)
     widened = states_ref[...].astype(jnp.float32)
     squared_average = jnp.mean(widened * widened, axis=-1, keepdims=True)
@@ -542,7 +542,7 @@
 
 
 def prepare(slot, gain, states, bases, downs, ups):
-    steps = 8
+    steps = 2
     seqs, decode, width = states.shape
     block = seqs // steps
 
@@ -559,8 +559,8 @@
         prepare_kernel,
         out_shape=(
             jax.ShapeDtypeStruct((seqs * decode, width), jnp.bfloat16),
-            jax.ShapeDtypeStruct((WROWS, QKV * steps), jnp.bfloat16),
-            jax.ShapeDtypeStruct((WROWS, OUT * steps), jnp.bfloat16),
+            jax.ShapeDtypeStruct((WROWS, QKV * 8), jnp.bfloat16),
+            jax.ShapeDtypeStruct((WROWS, OUT * 8), jnp.bfloat16),
         ),
         grid_spec=pltpu.PrefetchScalarGridSpec(
             num_scalar_prefetch=1,
@@ -574,8 +574,8 @@
             ],
             out_specs=(
                 pl.BlockSpec((block * decode, width), lambda i, s: (i, 0)),
-                pl.BlockSpec((WROWS, QKV), lambda i, s: (0, i)),
-                pl.BlockSpec((WROWS, OUT), lambda i, s: (0, lax.rem(i, 4) * 2 + i // 4)),
+                pl.BlockSpec((WROWS, QKV * 8 // steps), lambda i, s: (0, i)),
+                pl.BlockSpec((WROWS, OUT * 8 // steps), lambda i, s: (0, i)),
             ),
         ),
         name="prepare",

time: 138 us -> 128 us (0.928)
  the two profiles are of different devices: /device:TPU:92 before, /device:TPU:60 now
where the time goes in v4:
time: 128 us
  Pallas kernels  124 us (97%)
  local copies, waits for them, and re-layouts  1.85 us (1%)
  other arithmetic  1.8 us (1%)
    pallas_call x1, Pallas kernels, run_layer(): pl.pallas_call(layer_kernel, out_shape=jax.ShapeDtypeStruct((TOK // STEPS...  118 us
    pallas_call x1, Pallas kernels, prepare(): pl.pallas_call(prepare_kernel, out_shape=(jax.ShapeDtypeStruct((seqs * de...  6.13 us

profile of v4, /device:TPU:60, one launch (start us, length us, event | category | flops | bytes accessed | tf_op | source)
XLA Modules:
  0.0 128.2 jit_solution(4380945869244059752)
XLA Ops:
  0.7 0.7 convert_element_type.3
  1.3 0.1 iota_add_fusion
  1.4 0.1 add.23
  1.5 0.3 fusion
  1.8 0.7 pad_maximum_fusion
  2.6 6.1 %prepare.1 = (bf16[128,8192]{1,0:T(8,128)(2,1)}, bf16[64,10240]{1,0:T(8,128)(2,1)}, bf16[64,8192]{1,0:T(8,128)(2,1)}) custom-call(s32[1]{0:T(128)S(6)} %copy.20.slot_ref, f32[1,8192]{1,0:T(1,128)} %bitcast.5, bf16[32,4,8192]{2,1,0:T(4,128)(2,1)} %states_ref.1, bf16[64,8192]{1,0:T(8,128)(2,1)} %q_ref.1, bf16[64,1024]{1,0:T(8,128)(2,1)} %k_ref.1, ...), custom_call_target="tpu_custom_call" | custom-call | tf_op jit(solution)/shard_map/prepare/pallas_call | solution.py:558
  8.7 117.8 %layer.1 = bf16[32,4,1024]{2,1,0:T(4,128)(2,1)} custom-call(bf16[128,8192]{1,0:T(8,128)(2,1)} %get-tuple-element.8.a_ref, bf16[64,10240]{1,0:T(8,128)(2,1)} %get-tuple-element.9.w_ref, bf16[64,8192]{1,0:T(8,128)(2,1)} %get-tuple-element.10.o_ref, f32[128,128]{1,0:T(8,128)} %get-tuple-element.14.cos_ref, f32[128,128]{1,0:T(8,128)} %get-tuple-element.15.sin_ref, ...), custom_call_target="tpu_custom_call" | custom-call | tf_op jit(solution)/shard_map/layer/pallas_call | solution.py:482
  126.5 1.7 %copy.21 = bf16[32,4,1024]{2,1,0:T(4,128)(2,1)} copy(bf16[32,4,1024]{2,1,0:T(4,128)(2,1)} %layer.1) | data formatting | bytes 524288
  (1 shorter events, 0.0 us)

commit v5 on v4

--- a/solution.py
+++ b/solution.py
@@ -60,8 +60,8 @@
 
 def layer_kernel(
     a_ref, w_ref, o_ref, cos_ref, sin_ref, len_ref, k_ref, v_ref, out_ref,
-    abuf, wbuf, acc, crecv, ostage, wo_ref, kbuf, vbuf, qbuf, knew, vnew, mixed, heads, hbuf, dsend, drecv,
-    a_ss, a_rs, w1_ss, w1_rs, w2_ss, w2_rs, w3_ss, w3_rs, c_ss, c_rs,
+    abuf, wbuf, acc, cx, crecv, ostage, wo_ref, kbuf, vbuf, qbuf, knew, vnew, mixed, heads, hbuf, dsend, drecv,
+    a_ss, a_rs, w1_ss, w1_rs, w2_ss, w2_rs, w3_ss, w3_rs, cx_ss, cx_rs, c_ss, c_rs,
     o1_ss, o1_rs, r1_ss, r1_rs, r2_ss, r2_rs, r3_ss, r3_rs,
     kv_s, h_ss, h_rs, d_ss, d_rs,
 ):
@@ -201,8 +201,22 @@
         ref = wbuf.at[k, pl.ds(group_base(g, 1 - c), 4)]
         remote(ref, ref, w3_ss.at[k, g], w3_rs.at[k, g], cpart).wait_recv()
 
-    def c_copy(ch, e):
-        return remote(acc.at[ch, e], crecv.at[ch, e - 1], c_ss.at[ch, e], c_rs.at[ch, e], z_peer(e))
+    near = (1, 3)
+
+    def cx_copy(ch, k):
+        return remote(acc.at[ch, 2, k], cx.at[ch, k], cx_ss.at[ch, k], cx_rs.at[ch, k], z_peer(near[k]))
+
+    def c_copy(ch, n, k):
+        return remote(
+            acc.at[ch, near[n], k], crecv.at[ch, n, k], c_ss.at[ch, n, k], c_rs.at[ch, n, k], z_peer(near[n])
+        )
+
+    def combine(ch):
+        for k in range(2):
+            cx_copy(ch, k).wait_recv()
+            n = 1 - k
+            acc[ch, near[n], k] = acc[ch, near[n], k] + cx[ch, k]
+            c_copy(ch, n, k).start()
 
     def start_w1(ch, carry):
         for d in range(8):
@@ -241,9 +255,12 @@
             w3_wait(ch, g)
         rows = abuf[...].reshape(4 * TOK, PLANE)
         part = jnp.dot(rows, wbuf[ch].reshape(PLANE, CW), preferred_element_type=jnp.float32)
-        acc[ch] = part.reshape(4, TOK, CW)
-        for e in (1, 3, 2):
-            c_copy(ch, e).start()
+        part = part.reshape(4, TOK, CW)
+        acc[ch, :, 0] = part[:, :, :DH]
+        acc[ch, :, 1] = part[:, :, DH:]
+        for k in range(2):
+            cx_copy(ch, k).start()
+            c_copy(ch, k, k).start()
 
     def spread(d):
         o1_wait(d)
@@ -282,29 +299,34 @@
     for e in (1, 3, 2):
         a_copy(e).wait_recv()
     multiply(0)
-    share(3)
     multiply(1)
     forward(0)
     keep(0)
     multiply(2)
+    combine(0)
+    share(3)
     forward(1)
     keep(1)
     multiply(3)
+    combine(1)
     share(4)
     multiply(4)
     forward(3)
     keep(3)
+    combine(2)
     forward(2)
     keep(2)
+    combine(3)
+    combine(4)
 
     def rope(values):
         return values * cos_ref[...] + pltpu.roll(values, DH // 2, axis=1) * sin_ref[...]
 
     for ch in range(NC):
-        for e in range(1, 4):
-            c_copy(ch, e).wait_recv()
-        part = acc[ch, 0] + crecv[ch, 0] + crecv[ch, 1] + crecv[ch, 2]
-        first, second = part[:, :DH], part[:, DH:]
+        for n in range(2):
+            for k in range(2):
+                c_copy(ch, n, k).wait_recv()
+        first, second = [acc[ch, 0, k] + crecv[ch, 0, k] + crecv[ch, 1, k] for k in range(2)]
         if ch < NC - 1:
             qbuf[2 * ch] = rope(first).astype(jnp.bfloat16).astype(jnp.float32)
             qbuf[2 * ch + 1] = rope(second).astype(jnp.bfloat16).astype(jnp.float32)
@@ -458,8 +480,10 @@
             w2_copy(ch, g).wait_send()
         for g in range(4):
             w3_copy(ch, g).wait_send()
-        for e in range(1, 4):
-            c_copy(ch, e).wait_send()
+        for k in range(2):
+            cx_copy(ch, k).wait_send()
+            for n in range(2):
+                c_copy(ch, n, k).wait_send()
         return carry
 
     lax.fori_loop(0, NC, drain, 0)
@@ -487,8 +511,9 @@
         scratch_shapes=[
             pltpu.VMEM((4, TOK, PLANE), jnp.bfloat16),
             pltpu.VMEM((NC, 32, WROWS, CW), jnp.bfloat16),
-            pltpu.VMEM((NC, 4, TOK, CW), jnp.float32),
-            pltpu.VMEM((NC, 3, TOK, CW), jnp.float32),
+            pltpu.VMEM((NC, 4, 2, TOK, DH), jnp.float32),
+            pltpu.VMEM((NC, 2, TOK, DH), jnp.float32),
+            pltpu.VMEM((NC, 2, 2, TOK, DH), jnp.float32),
             pltpu.VMEM((WROWS, 2 * OUT), jnp.bfloat16),
             pltpu.VMEM((32, WROWS, 2 * OUT), jnp.bfloat16),
             pltpu.VMEM(keys.shape, jnp.bfloat16),
@@ -505,7 +530,8 @@
             DMA((NC, 8)), DMA((NC, 8)),
             DMA((NC, 2)), DMA((NC, 2)),
             DMA((NC, 4)), DMA((NC, 4)),
-            DMA((NC, 4)), DMA((NC, 4)),
+            DMA((NC, 2)), DMA((NC, 2)),
+            DMA((NC, 2, 2)), DMA((NC, 2, 2)),
             DMA((4,)), DMA((4,)),
             DMA((2, 4)), DMA((2, 4)),
             DMA((4,)), DMA((4,)),

time: 128 us -> 123 us (0.961)
  Pallas kernels: 124 us -> 118 us
    pallas_call x1, Pallas kernels: 118 us -> 112 us  [run_layer(): pl.pallas_call(layer_kernel, out_shape=jax.ShapeDtypeStruct((TOK // STEPS...]
where the time goes in v5:
time: 123 us
  Pallas kernels  118 us (96%)
  local copies, waits for them, and re-layouts  1.85 us (2%)
  other arithmetic  1.8 us (1%)
    pallas_call x1, Pallas kernels, run_layer(): pl.pallas_call(layer_kernel, out_shape=jax.ShapeDtypeStruct((TOK // STEPS...  112 us
    pallas_call x1, Pallas kernels, prepare(): pl.pallas_call(prepare_kernel, out_shape=(jax.ShapeDtypeStruct((seqs * de...  6.13 us

profile of v5, /device:TPU:60, one launch (start us, length us, event | category | flops | bytes accessed | tf_op | source)
XLA Modules:
  0.0 122.8 jit_solution(11799053172437295268)
XLA Ops:
  0.7 0.7 convert_element_type.3
  1.3 0.1 iota_add_fusion
  1.4 0.1 add.23
  1.5 0.3 fusion
  1.8 0.7 pad_maximum_fusion
  2.6 6.1 %prepare.1 = (bf16[128,8192]{1,0:T(8,128)(2,1)}, bf16[64,10240]{1,0:T(8,128)(2,1)}, bf16[64,8192]{1,0:T(8,128)(2,1)}) custom-call(s32[1]{0:T(128)S(6)} %copy.20.slot_ref, f32[1,8192]{1,0:T(1,128)} %bitcast.5, bf16[32,4,8192]{2,1,0:T(4,128)(2,1)} %states_ref.1, bf16[64,8192]{1,0:T(8,128)(2,1)} %q_ref.1, bf16[64,1024]{1,0:T(8,128)(2,1)} %k_ref.1, ...), custom_call_target="tpu_custom_call" | custom-call | tf_op jit(solution)/shard_map/prepare/pallas_call | solution.py:584
  8.7 112.3 %layer.1 = bf16[32,4,1024]{2,1,0:T(4,128)(2,1)} custom-call(bf16[128,8192]{1,0:T(8,128)(2,1)} %get-tuple-element.8.a_ref, bf16[64,10240]{1,0:T(8,128)(2,1)} %get-tuple-element.9.w_ref, bf16[64,8192]{1,0:T(8,128)(2,1)} %get-tuple-element.10.o_ref, f32[128,128]{1,0:T(8,128)} %get-tuple-element.14.cos_ref, f32[128,128]{1,0:T(8,128)} %get-tuple-element.15.sin_ref, ...), custom_call_target="tpu_custom_call" | custom-call | tf_op jit(solution)/shard_map/layer/pallas_call | solution.py:506
  121.0 1.7 %copy.21 = bf16[32,4,1024]{2,1,0:T(4,128)(2,1)} copy(bf16[32,4,1024]{2,1,0:T(4,128)(2,1)} %layer.1) | data formatting | bytes 524288
  (1 shorter events, 0.0 us)

commit v6 on v5

--- a/solution.py
+++ b/solution.py
@@ -386,7 +386,7 @@
             attend_pair(qt * 4 + n)
         rows = pl.ds(pl.multiple_of(qt * QT, QT), QT)
         heads[rows] = mixed[rows].astype(jnp.bfloat16)
-        for d in (2, 1, 3):
+        for d in (1, 3, 2):
             h_send(qt, d).start()
 
         @pl.when(here)

time: 123 us -> 121 us (0.984)
  Pallas kernels: 118 us -> 116 us
    pallas_call x1, Pallas kernels: 112 us -> 110 us  [run_layer(): pl.pallas_call(layer_kernel, out_shape=jax.ShapeDtypeStruct((TOK // STEPS...]
where the time goes in v6:
time: 121 us
  Pallas kernels  116 us (96%)
  local copies, waits for them, and re-layouts  1.85 us (2%)
  other arithmetic  1.8 us (1%)
    pallas_call x1, Pallas kernels, run_layer(): pl.pallas_call(layer_kernel, out_shape=jax.ShapeDtypeStruct((TOK // STEPS...  110 us
    pallas_call x1, Pallas kernels, prepare(): pl.pallas_call(prepare_kernel, out_shape=(jax.ShapeDtypeStruct((seqs * de...  6.13 us

profile of v6, /device:TPU:60, one launch (start us, length us, event | category | flops | bytes accessed | tf_op | source)
XLA Modules:
  0.0 120.6 jit_solution(4891652746784452795)
XLA Ops:
  0.7 0.7 convert_element_type.3
  1.3 0.1 iota_add_fusion
  1.4 0.1 add.23
  1.5 0.3 fusion
  1.8 0.7 pad_maximum_fusion
  2.6 6.1 %prepare.1 = (bf16[128,8192]{1,0:T(8,128)(2,1)}, bf16[64,10240]{1,0:T(8,128)(2,1)}, bf16[64,8192]{1,0:T(8,128)(2,1)}) custom-call(s32[1]{0:T(128)S(6)} %copy.20.slot_ref, f32[1,8192]{1,0:T(1,128)} %bitcast.5, bf16[32,4,8192]{2,1,0:T(4,128)(2,1)} %states_ref.1, bf16[64,8192]{1,0:T(8,128)(2,1)} %q_ref.1, bf16[64,1024]{1,0:T(8,128)(2,1)} %k_ref.1, ...), custom_call_target="tpu_custom_call" | custom-call | tf_op jit(solution)/shard_map/prepare/pallas_call | solution.py:584
  8.7 110.1 %layer.1 = bf16[32,4,1024]{2,1,0:T(4,128)(2,1)} custom-call(bf16[128,8192]{1,0:T(8,128)(2,1)} %get-tuple-element.8.a_ref, bf16[64,10240]{1,0:T(8,128)(2,1)} %get-tuple-element.9.w_ref, bf16[64,8192]{1,0:T(8,128)(2,1)} %get-tuple-element.10.o_ref, f32[128,128]{1,0:T(8,128)} %get-tuple-element.14.cos_ref, f32[128,128]{1,0:T(8,128)} %get-tuple-element.15.sin_ref, ...), custom_call_target="tpu_custom_call" | custom-call | tf_op jit(solution)/shard_map/layer/pallas_call | solution.py:506
  118.8 1.7 %copy.21 = bf16[32,4,1024]{2,1,0:T(4,128)(2,1)} copy(bf16[32,4,1024]{2,1,0:T(4,128)(2,1)} %layer.1) | data formatting | bytes 524288
  (1 shorter events, 0.0 us)
